TPU v7x, 256 devices: a whole 4x4x8 slice. The times are simulated.
256 devices in a mesh: dp: 8 (over y, core), expert: 32 (over z, x).
Axes of the slice: x: 4, y: 4, z: 8, core: 2. Of those that a mesh axis runs over, the one named last changes fastest.
Arguments:
- tokens: bfloat16 [32768, 2560], P(('dp', 'expert')), may hold values from -6 to 6
- cotangent: bfloat16 [32768, 2560], P(('dp', 'expert')), may hold values from -6 to 6
- routes: int32 [32768, 1], P(('dp', 'expert')), may hold values from 0 to 31; in each aligned block of 128 rows (0 to 127, 128 to 255, ...) at most 6 rows name the same one
- gates: float32 [32768, 1], P(('dp', 'expert')), may hold values from 0.25 to 1
- hot_index: int32 [4096], P(('dp', 'expert')), may hold values from 0 to 127, as said below
- hot_gate: float32 [4096], P(('dp', 'expert')), may hold values from 0.25 to 1
- w_gate_up: bfloat16 [32, 2560, 1536], P('expert', 'dp'), may hold values from -0.125 to 0.125
- w_down: bfloat16 [32, 768, 2560], P('expert', 'dp'), may hold values from -0.21875 to 0.21875
- w_hot_gu: bfloat16 [2, 768, 2560], P(None, 'dp', 'expert'), may hold values from -0.125 to 0.125
- w_hot_dn: bfloat16 [768, 2560], P('dp', 'expert'), may hold values from -0.21875 to 0.21875
Outputs:
- layer_out: bfloat16 [32768, 2560], P(('dp', 'expert'))
- input_grad: bfloat16 [32768, 2560], P(('dp', 'expert'))
- grad_gate_up: bfloat16 [32, 2560, 1536], P('expert', 'dp')
- grad_down: bfloat16 [32, 768, 2560], P('expert', 'dp')
- grad_hot_gu: bfloat16 [2, 768, 2560], P(None, 'dp', 'expert')
- grad_hot_dn: bfloat16 [768, 2560], P('dp', 'expert')
Inputs may be any that keep to these rules, and one draw needn't show every extreme that they name: `routes`: each token names 1 different routed experts; the tokens of one device name any one routed expert at most 6 times, some expert exactly 6 times. `hot_index`: the 16 entries of one device name different tokens of that device, by their index within the device.
All inputs are finite; a program needn't handle non-finite values.
Results may differ from a plain program's by a relative error of at most 0.018.
Values may be sent and summed in bfloat16 or wider, within the bound.
A program may use at most 128 MiB of HBM per device.

v0:
```python
import jax
import jax.numpy as jnp
from jax import lax
from jax.sharding import PartitionSpec as P


def slot_positions(route_block, count):
    flat = route_block.reshape(-1)
    onehot = (flat[:, None] == jnp.arange(count, dtype=jnp.int32)[None, :]).astype(jnp.int32)
    before = jnp.cumsum(onehot, axis=0) - onehot
    return (flat, jnp.sum(before * onehot, axis=1))


def expert_forward(rows_x, w_gu):
    width = w_gu.shape[1] // 2
    act = jnp.dot(rows_x, w_gu, preferred_element_type=jnp.float32)
    gate_part = act[:, :width]
    up_part = act[:, width:]
    hidden = (gate_part * jax.nn.sigmoid(gate_part) * up_part).astype(jnp.bfloat16)
    return (act, hidden)


def expert_output(hidden, w_dn):
    return jnp.dot(hidden, w_dn, preferred_element_type=jnp.float32).astype(jnp.bfloat16)


def expert_delta(scaled_rows, act, w_gu, w_dn):
    width = w_gu.shape[1] // 2
    gate_part = act[:, :width]
    up_part = act[:, width:]
    sigma = jax.nn.sigmoid(gate_part)
    d_hidden = lax.dot_general(
        scaled_rows, w_dn, (((1,), (1,)), ((), ())), preferred_element_type=jnp.float32
    )
    d_gate = d_hidden * up_part * sigma * (1.0 + gate_part * (1.0 - sigma))
    d_up = d_hidden * gate_part * sigma
    d_act = jnp.concatenate([d_gate, d_up], axis=1).astype(jnp.bfloat16)
    d_rows = lax.dot_general(
        d_act, w_gu, (((1,), (1,)), ((), ())), preferred_element_type=jnp.float32
    ).astype(jnp.bfloat16)
    return (d_act, d_rows)


def local(
    tokens, cotangent, routes, gates, hot_index, hot_gate, w_gate_up, w_down, w_hot_gu, w_hot_dn
):
    owners = lax.axis_size("expert")
    groups = lax.axis_size("dp")
    tok_dev, width_d = tokens.shape
    topk = routes.shape[1]
    slots = max(2, 3 * tok_dev * topk // (2 * owners))
    entries = tok_dev * topk
    inverse = 1.0 / (4 * groups)
    feature_dims = (((1,), (1,)), ((), ()))
    row_dims = (((0,), (0,)), ((), ()))
    hot_x = tokens[hot_index]
    hot_s = (hot_gate[:, None] * cotangent[hot_index].astype(jnp.float32)).astype(jnp.bfloat16)
    slice_gu, slice_dn = (
        lax.all_gather(w_hot_gu, "expert", axis=2, tiled=True),
        lax.all_gather(w_hot_dn, "expert", axis=1, tiled=True),
    )
    all_x, all_s = (
        lax.all_gather(hot_x, "dp", axis=0, tiled=True),
        lax.all_gather(hot_s, "dp", axis=0, tiled=True),
    )
    hot_g = lax.dot_general(all_x, slice_gu[0], feature_dims, preferred_element_type=jnp.float32)
    hot_u = lax.dot_general(all_x, slice_gu[1], feature_dims, preferred_element_type=jnp.float32)
    hot_sigma = jax.nn.sigmoid(hot_g)
    hot_hidden = (hot_g * hot_sigma * hot_u).astype(jnp.bfloat16)
    hot_dh = lax.dot_general(all_s, slice_dn, feature_dims, preferred_element_type=jnp.float32)
    hot_dg = (hot_dh * hot_u * hot_sigma * (1.0 + hot_g * (1.0 - hot_sigma))).astype(jnp.bfloat16)
    hot_du = (hot_dh * hot_g * hot_sigma).astype(jnp.bfloat16)
    out_rows = jnp.dot(hot_hidden, slice_dn, preferred_element_type=jnp.float32)
    grad_rows = jnp.dot(hot_dg, slice_gu[0], preferred_element_type=jnp.float32) + jnp.dot(
        hot_du, slice_gu[1], preferred_element_type=jnp.float32
    )
    hot_back = lax.psum_scatter(
        jnp.stack([out_rows, grad_rows], axis=1).astype(jnp.bfloat16),
        "dp",
        scatter_dimension=0,
        tiled=True,
    ).astype(jnp.float32)
    part_hot_gu = (
        jnp.stack(
            [
                lax.dot_general(hot_dg, all_x, row_dims, preferred_element_type=jnp.float32),
                lax.dot_general(hot_du, all_x, row_dims, preferred_element_type=jnp.float32),
            ]
        )
        * inverse
    )
    part_hot_dn = (
        lax.dot_general(hot_hidden, all_s, row_dims, preferred_element_type=jnp.float32) * inverse
    )
    grad_hot_gu, grad_hot_dn = (
        lax.psum_scatter(
            part_hot_gu.astype(jnp.bfloat16), "expert", scatter_dimension=2, tiled=True
        ).astype(jnp.float32),
        lax.psum_scatter(
            part_hot_dn.astype(jnp.bfloat16), "expert", scatter_dimension=1, tiled=True
        ).astype(jnp.float32),
    )
    flat, pos = slot_positions(routes, owners)
    dest = flat * slots + pos
    entry_ids = jnp.arange(entries, dtype=jnp.int32)
    table = jnp.full((owners * slots,), entries, jnp.int32).at[dest].set(entry_ids)
    scaled = (gates[:, :, None] * cotangent[:, None, :].astype(jnp.float32)).astype(jnp.bfloat16)
    scaled_pad = jnp.concatenate(
        [scaled.reshape(entries, width_d), jnp.zeros((1, width_d), jnp.bfloat16)], axis=0
    )
    x_pad = jnp.concatenate([tokens, jnp.zeros((1, width_d), jnp.bfloat16)], axis=0)
    send_x = x_pad[table // topk].reshape(owners, slots, width_d)
    send_s = scaled_pad[table].reshape(owners, slots, width_d)
    whole_gu, whole_dn = (
        lax.all_gather(w_gate_up, "dp", axis=1, tiled=True),
        lax.all_gather(w_down, "dp", axis=1, tiled=True),
    )
    w_gu = whole_gu[0]
    w_dn = whole_dn[0]
    recv_x, recv_s = (
        lax.all_to_all(send_x, "expert", split_axis=0, concat_axis=0, tiled=True),
        lax.all_to_all(send_s, "expert", split_axis=0, concat_axis=0, tiled=True),
    )
    rows_x = recv_x.reshape(owners * slots, width_d)
    rows_s = recv_s.reshape(owners * slots, width_d)
    act, hidden = expert_forward(rows_x, w_gu)
    out = expert_output(hidden, w_dn).reshape(owners, slots, width_d)
    d_act, d_rows = expert_delta(rows_s, act, w_gu, w_dn)
    back_out, back_rows = (
        lax.all_to_all(out, "expert", split_axis=0, concat_axis=0, tiled=True),
        lax.all_to_all(
            d_rows.reshape(owners, slots, width_d),
            "expert",
            split_axis=0,
            concat_axis=0,
            tiled=True,
        ),
    )
    full_gu = lax.dot_general(rows_x, d_act, row_dims, preferred_element_type=jnp.float32) * inverse
    full_dn = (
        lax.dot_general(hidden, rows_s, row_dims, preferred_element_type=jnp.float32) * inverse
    )
    grad_gu, grad_dn = (
        lax.psum_scatter(
            full_gu.astype(jnp.bfloat16), "dp", scatter_dimension=0, tiled=True
        ).astype(jnp.float32),
        lax.psum_scatter(
            full_dn.astype(jnp.bfloat16), "dp", scatter_dimension=0, tiled=True
        ).astype(jnp.float32),
    )
    picked = back_out.reshape(owners * slots, width_d)[dest].astype(jnp.float32)
    layer_out = (
        (gates.reshape(entries)[:, None] * picked).reshape(tok_dev, topk, width_d).sum(axis=1)
    )
    layer_out = layer_out.at[hot_index].add(hot_gate[:, None] * hot_back[:, 0])
    returned = back_rows.reshape(owners * slots, width_d)[dest].astype(jnp.float32)
    input_grad = returned.reshape(tok_dev, topk, width_d).sum(axis=1)
    input_grad = input_grad.at[hot_index].add(hot_back[:, 1])
    return (
        layer_out.astype(jnp.bfloat16),
        input_grad.astype(jnp.bfloat16),
        grad_gu.astype(jnp.bfloat16)[None],
        grad_dn.astype(jnp.bfloat16)[None],
        grad_hot_gu.astype(jnp.bfloat16),
        grad_hot_dn.astype(jnp.bfloat16),
    )


def solution(mesh):
    placed = (
        P(("dp", "expert"), None),
        P(("dp", "expert"), None),
        P(("dp", "expert"), None),
        P(("dp", "expert"), None),
        P(("dp", "expert")),
        P(("dp", "expert")),
        P("expert", "dp", None),
        P("expert", "dp", None),
        P(None, "dp", "expert"),
        P("dp", "expert"),
    )
    return jax.shard_map(
        local,
        mesh=mesh,
        in_specs=placed,
        out_specs=(
            P(("dp", "expert"), None),
            P(("dp", "expert"), None),
            P("expert", "dp", None),
            P("expert", "dp", None),
            P(None, "dp", "expert"),
            P("dp", "expert"),
        ),
        check_vma=False,
    )
```

profile of v0, /device:TPU:7, one launch (start us, length us, event | category | flops | bytes accessed | tf_op | source)
XLA Modules:
  0.0 533.8 jit_solution(6928361060983992948)
XLA Ops:
  8.1 0.7 all-gather.4.cloned.1.call-update
  8.8 0.7 all-gather.6.cloned.1.call-update
  9.7 0.2 reduce_window_sum.11
  9.8 0.2 select_reduce_fusion
  10.0 1.0 scatter_custom_fusion
  11.0 1.2 gather_fusion
  12.3 1.3 reshape.59
  13.5 11.2 %all-to-all-start = ((bf16[32,6,2560]{2,1,0:T(8,128)(2,1)}), bf16[32,6,2560]{2,1,0:T(8,128)(2,1)}, u32[]{:S(2)}, u32[]{:S(2)}) async-start(bf16[32,6,2560]{2,1,0:T(8,128)(2,1)} %reshape.59), calls=%async_computation | async-start | bytes 2621440 | tf_op jit(solution)/shard_map/all_to_all | solution.py:121
  24.8 0.6 gather_fusion.2
  25.5 0.6 gather_fusion.3
  26.1 61.8 %all_gather.22 = bf16[96,2560]{0,1:T(8,128)(2,1)S(1)} all-gather(bf16[96,80]{0,1:T(8,128)(2,1)S(1)} %copy-done.4), channel_id=1, replica_groups=mesh['dp'=8,'expert'=32] {'expert'}, dimensions={1}, use_global_device_ids=true | all-gather | bytes 506880 | tf_op jit(solution)/shard_map/all_gather | solution.py:60
  87.8 38.7 %all_gather.21 = bf16[2,96,2560]{1,2,0:T(8,128)(2,1)S(1)} all-gather(bf16[2,96,80]{1,2,0:T(8,128)(2,1)S(1)} %copy-done.3), channel_id=1, replica_groups=mesh['dp'=8,'expert'=32] {'expert'}, dimensions={2}, use_global_device_ids=true | all-gather | bytes 1013760 | tf_op jit(solution)/shard_map/all_gather | solution.py:59
  126.6 33.8 %all-gather = bf16[128,2560]{1,0:T(8,128)(2,1)S(1)} all-gather(bf16[16,2560]{1,0:T(8,128)(2,1)S(1)} %gather_fusion.2), channel_id=2, replica_groups=mesh['dp'=8,'expert'=32] {'dp'}, dimensions={0}, use_global_device_ids=true | all-gather | bytes 737280 | tf_op jit(solution)/shard_map/all_gather | solution.py:63
  160.3 0.4 fusion.20
  160.8 13.2 %all_gather.23 = bf16[128,2560]{1,0:T(8,128)(2,1)S(1)} all-gather(bf16[16,2560]{1,0:T(8,128)(2,1)S(1)} %multiply_convert_fusion.6), channel_id=1, replica_groups=mesh['dp'=8,'expert'=32] {'dp'}, dimensions={0}, use_global_device_ids=true | all-gather | bytes 737280 | tf_op jit(solution)/shard_map/all_gather | solution.py:64
  174.1 0.4 fusion.33
  174.5 0.4 multiply_convert_fusion.9
  174.9 0.3 convolution_bitcast_fusion
  175.2 0.3 convolution_bitcast_fusion.1
  175.5 1.1 fusion.18
  176.5 3.8 copy.18
  180.4 0.4 fusion.17
  180.8 0.4 fusion.19
  181.2 0.4 fusion.16
  181.5 1.3 pad_maximum_fusion
  182.8 0.6 copy-done.6
  183.4 0.2 multiply_convert_fusion.2
  183.7 1.2 gather_fusion.4
  184.9 1.3 reshape.63
  186.2 8.8 %all-to-all-start.2 = ((bf16[32,6,2560]{2,1,0:T(8,128)(2,1)}), bf16[32,6,2560]{2,1,0:T(8,128)(2,1)S(1)}, u32[]{:S(2)}, u32[]{:S(2)}) async-start(bf16[32,6,2560]{2,1,0:T(8,128)(2,1)} %reshape.63), calls=%async_computation.3 | async-start | bytes 2621440 | tf_op jit(solution)/shard_map/all_to_all | solution.py:122
  195.0 1.2 fusion.15
  196.3 0.2 reduce-scatter.9.cloned.1.call-start
  196.5 1.5 reshape.60
  198.0 37.2 %all-to-all-done.2 = bf16[32,6,2560]{2,1,0:T(8,128)(2,1)S(1)} async-done(((bf16[32,6,2560]{2,1,0:T(8,128)(2,1)}), bf16[32,6,2560]{2,1,0:T(8,128)(2,1)S(1)}, u32[]{:S(2)}, u32[]{:S(2)}) %all-to-all-start.2) | async-done | bytes 983072 | tf_op jit(solution)/shard_map/all_to_all | solution.py:122
  235.2 1.1 reshape.64
  236.3 6.0 %fusion.2 = f32[192,1536]{1,0:T(8,128)} fusion(bf16[192,2560]{1,0:T(8,128)(2,1)S(1)} %reshape.60, bf16[1,2560,1536]{2,1,0:T(8,128)(2,1)} %all-gather.4.cloned.1.call-done), kind=kOutput, calls=%fused_computation.12 | convolution fusion | flops 1509949440 | bytes 10027008 | tf_op jit(solution)/shard_map/dot_general | solution.py:16
  242.4 3.9 multiply_convert_fusion.4
  246.3 3.2 multiply_convert_fusion.1
  249.6 5.4 %multiply_convert_fusion = bf16[2560,1536]{1,0:T(8,128)(2,1)} fusion(bf16[192,2560]{1,0:T(8,128)(2,1)S(1)} %reshape.60, bf16[192,768]{1,0:T(8,128)(2,1)S(1)} %get-tuple-element.25, bf16[192,768]{1,0:T(8,128)(2,1)S(1)} %get-tuple-element.24), kind=kOutput, calls=%fused_computation.9 | convolution fusion | flops 1518993408 | bytes 9437184 | tf_op jit(solution)/shard_map/dot_general | solution.py:139
  255.0 3.1 fusion.8
  258.1 1.3 reshape.61
  259.3 6.0 %all-to-all-start.1 = ((bf16[32,6,2560]{2,1,0:T(8,128)(2,1)}), bf16[32,6,2560]{2,1,0:T(8,128)(2,1)S(1)}, u32[]{:S(2)}, u32[]{:S(2)}) async-start(bf16[32,6,2560]{2,1,0:T(8,128)(2,1)} %reshape.61), calls=%async_computation.1 | async-start | bytes 2621440 | tf_op jit(solution)/shard_map/all_to_all | solution.py:130
  265.4 5.9 %fusion.11 = bf16[192,2560]{1,0:T(8,128)(2,1)S(1)} fusion(bf16[1,2560,1536]{2,1,0:T(8,128)(2,1)} %all-gather.4.cloned.1.call-done, bf16[192,768]{1,0:T(8,128)(2,1)S(1)} %get-tuple-element.25, bf16[192,768]{1,0:T(8,128)(2,1)S(1)} %get-tuple-element.24), kind=kOutput, calls=%fused_computation.20 | convolution fusion | flops 1511620608 | bytes 9437184 | tf_op jit(solution)/shard_map/dot_general | solution.py:38
  271.3 1.3 reshape.65
  272.6 27.6 %all-to-all-done.1 = bf16[32,6,2560]{2,1,0:T(8,128)(2,1)S(1)} async-done(((bf16[32,6,2560]{2,1,0:T(8,128)(2,1)}), bf16[32,6,2560]{2,1,0:T(8,128)(2,1)S(1)}, u32[]{:S(2)}, u32[]{:S(2)}) %all-to-all-start.1) | async-done | bytes 983072 | tf_op jit(solution)/shard_map/all_to_all | solution.py:130
  300.2 5.6 %all-to-all-start.3 = ((bf16[32,6,2560]{2,1,0:T(8,128)(2,1)}), bf16[32,6,2560]{2,1,0:T(8,128)(2,1)}, u32[]{:S(2)}, u32[]{:S(2)}) async-start(bf16[32,6,2560]{2,1,0:T(8,128)(2,1)} %reshape.65), calls=%async_computation.4 | async-start | bytes 2621440 | tf_op jit(solution)/shard_map/all_to_all | solution.py:131
  305.9 0.6 dynamic-slice
  307.1 40.3 %all-reduce.5.cloned.1.call-done = bf16[2,96,2560]{1,0,2:T(2,128)(2,1)} async-done(((bf16[2,96,2560]{1,0,2:T(2,128)(2,1)}), bf16[2,96,2560]{1,0,2:T(2,128)(2,1)}) %all-reduce.5.cloned.1.call-update) | async-done | bytes 983056
  347.4 0.8 constant_dynamic-slice_fusion
  348.2 0.6 copy.19
  348.8 0.9 convert_element_type.85
  349.8 0.4 reshape.62
  350.2 1.0 gather_fusion.1
  351.1 0.2 convert_multiply_fusion
  351.3 1.4 scatter_custom_fusion.1
  352.7 0.9 convert_element_type.86
  353.6 1.5 reshape.66
  355.1 1.0 gather_fusion.5
  356.0 0.1 convert_element_type.90
  356.2 1.3 scatter_custom_fusion.2
  357.5 0.9 convert_element_type.91
  358.4 66.3 %reduce-scatter.11.cloned.1.call-done = bf16[96,80]{0,1:T(8,128)(2,1)} async-done(((bf16[96,2560]{0,1:T(8,128)(2,1)}), bf16[96,80]{0,1:T(8,128)(2,1)}) %reduce-scatter.11.cloned.1.call-update) | async-done | bytes 15376 | tf_op jit(solution)/shard_map/reduce_scatter | solution.py:99
  424.7 44.8 %reduce-scatter.9.cloned.1.call-done = bf16[96,2560]{1,0:T(8,128)(2,1)} async-done(((bf16[768,2560]{1,0:T(8,128)(2,1)}), bf16[96,2560]{1,0:T(8,128)(2,1)}) %reduce-scatter.9.cloned.1.call-update) | async-done | bytes 491536 | tf_op jit(solution)/shard_map/reduce_scatter | solution.py:147
  469.5 56.8 %reduce-scatter.7.cloned.1.call-done = bf16[320,1536]{1,0:T(8,128)(2,1)} async-done(((bf16[2560,1536]{1,0:T(8,128)(2,1)}), bf16[320,1536]{1,0:T(8,128)(2,1)}) %reduce-scatter.7.cloned.1.call-update) | async-done | bytes 983056 | tf_op jit(solution)/shard_map/reduce_scatter | solution.py:144
  (46 shorter events, 0.7 us)
Async XLA Ops:
  8.0 1.5 copy-start
  8.0 1.6 copy-start.5
  8.0 228.3 %all-gather.4.cloned.1.call-start = ((), (), s32[]{:S(2)}) async-start(), calls=%async_computation.8 | async-start | bytes 8847360 | tf_op jit(solution)/shard_map/all_gather | solution.py:115
  8.8 233.6 %all-gather.6.cloned.1.call-start = ((), (), s32[]{:S(2)}) async-start(), calls=%async_computation.9 | async-start | bytes 4423680 | tf_op jit(solution)/shard_map/all_gather | solution.py:116
  13.5 11.3 %copy-start.8 = (s32[16]{0:T(128)S(1)}, s32[16]{0:T(128)}, u32[]{:S(2)}) copy-start(s32[16]{0:T(128)} %param.14) | copy-start | bytes 196
  13.5 11.9 %copy-start.1 = (bf16[128,2560]{1,0:T(8,128)(2,1)S(1)}, bf16[128,2560]{1,0:T(8,128)(2,1)}, u32[]{:S(2)}) copy-start(bf16[128,2560]{1,0:T(8,128)(2,1)} %param.11) | copy-start | bytes 1966084
  13.5 172.6 %all-to-all-start = ((bf16[32,6,2560]{2,1,0:T(8,128)(2,1)}), bf16[32,6,2560]{2,1,0:T(8,128)(2,1)}, u32[]{:S(2)}, u32[]{:S(2)}) async-start(bf16[32,6,2560]{2,1,0:T(8,128)(2,1)} %reshape.59), calls=%async_computation | async-start | bytes 2621440 | tf_op jit(solution)/shard_map/all_to_all | solution.py:121
  24.7 1.3 copy-start.4
  24.7 63.1 %copy-start.3 = (bf16[2,96,80]{1,2,0:T(8,128)(2,1)S(1)}, bf16[2,96,80]{1,2,0:T(8,128)(2,1)}, u32[]{:S(2)}) copy-start(bf16[2,96,80]{1,2,0:T(8,128)(2,1)} %param.18) | copy-start | bytes 92164
  24.8 322.6 %all-reduce.5.cloned.1.call-start = ((), (), s32[]{:S(2)}) async-start(), calls=%async_computation.14 | async-start | bytes 2621440
  126.6 34.2 %copy-start.7 = (f32[16]{0:T(128)S(1)}, f32[16]{0:T(128)}, u32[]{:S(2)}) copy-start(f32[16]{0:T(128)} %param.15) | copy-start | bytes 196
  180.4 168.5 %reduce-scatter.5.cloned.1.call-start = ((), (), s32[]{:S(2)}) async-start(), calls=%async_computation.10 | async-start | bytes 1474560 | tf_op jit(solution)/shard_map/reduce_scatter | solution.py:77
  182.8 0.7 copy-start.6
  186.2 49.1 %all-to-all-start.2 = ((bf16[32,6,2560]{2,1,0:T(8,128)(2,1)}), bf16[32,6,2560]{2,1,0:T(8,128)(2,1)S(1)}, u32[]{:S(2)}, u32[]{:S(2)}) async-start(bf16[32,6,2560]{2,1,0:T(8,128)(2,1)} %reshape.63), calls=%async_computation.3 | async-start | bytes 2621440 | tf_op jit(solution)/shard_map/all_to_all | solution.py:122
  195.0 229.8 %reduce-scatter.11.cloned.1.call-start = ((), (), s32[]{:S(2)}) async-start(), calls=%async_computation.13 | async-start | bytes 675840 | tf_op jit(solution)/shard_map/reduce_scatter | solution.py:99
  196.3 273.2 %reduce-scatter.9.cloned.1.call-start = ((), (), s32[]{:S(2)}) async-start(), calls=%async_computation.12 | async-start | bytes 4423680 | tf_op jit(solution)/shard_map/reduce_scatter | solution.py:147
  236.3 6.1 %copy-start.2 = (bf16[192,2560]{1,0:T(8,128)(2,1)S(1)}, bf16[192,2560]{1,0:T(8,128)(2,1)}, u32[]{:S(2)}) copy-start(bf16[192,2560]{1,0:T(8,128)(2,1)} %reshape.64) | copy-start | bytes 2949124
  249.5 276.8 %reduce-scatter.7.cloned.1.call-start = ((), (), s32[]{:S(2)}) async-start(), calls=%async_computation.11 | async-start | bytes 8847360 | tf_op jit(solution)/shard_map/reduce_scatter | solution.py:144
  259.3 40.9 %all-to-all-start.1 = ((bf16[32,6,2560]{2,1,0:T(8,128)(2,1)}), bf16[32,6,2560]{2,1,0:T(8,128)(2,1)S(1)}, u32[]{:S(2)}, u32[]{:S(2)}) async-start(bf16[32,6,2560]{2,1,0:T(8,128)(2,1)} %reshape.61), calls=%async_computation.1 | async-start | bytes 2621440 | tf_op jit(solution)/shard_map/all_to_all | solution.py:130
  272.6 33.3 %copy-start.9 = (u32[256]{0:T(256)S(1)}, u32[256]{0:T(256)}, u32[]{:S(2)}) copy-start(u32[256]{0:T(256)} %constant.56) | copy-start | bytes 3076
  300.2 53.4 %all-to-all-start.3 = ((bf16[32,6,2560]{2,1,0:T(8,128)(2,1)}), bf16[32,6,2560]{2,1,0:T(8,128)(2,1)}, u32[]{:S(2)}, u32[]{:S(2)}) async-start(bf16[32,6,2560]{2,1,0:T(8,128)(2,1)} %reshape.65), calls=%async_computation.4 | async-start | bytes 2621440 | tf_op jit(solution)/shard_map/all_to_all | solution.py:131
Sparse Core Ops, SparseCore 0:
  10.7 53.3 all-gather.3
  65.9 33.6 all-gather.5
  183.7 32.6 reduce-scatter.4
  220.5 204.2 reduce-scatter.10
  427.7 41.7 reduce-scatter.8
  472.5 53.7 reduce-scatter.6
Sparse Core Ops, SparseCore 1:
  180.5 166.9 all-reduce.4
where the time goes:
time: 536 us; the launch traced here: 534 us
  waiting for transfers between devices  275 us (51%)
  blocking collectives  148 us (28%)
  starting transfers between devices  32.1 us (6%)
  matrix products  31.6 us (6%)
  local copies, waits for them, and re-layouts  22.6 us (4%)
  between operations  16.6 us (3%)
  other arithmetic  8.81 us (2%)
    reduce_scatter x1, waiting for transfers between devices, local(): lax.psum_scatter(part_hot_dn.astype(jnp.bfloat16), 'expert', scatter_dime...  66.3 us
    all_gather x1, blocking collectives, local(): lax.all_gather(w_hot_dn, 'expert', axis=1, tiled=True)  61.8 us
    reduce_scatter x1, waiting for transfers between devices, local(): lax.psum_scatter(full_gu.astype(jnp.bfloat16), 'dp', scatter_dimension=0,...  56.8 us
    reduce_scatter x1, waiting for transfers between devices, local(): lax.psum_scatter(full_dn.astype(jnp.bfloat16), 'dp', scatter_dimension=0,...  44.8 us
    unnamed x8, waiting for transfers between devices  41.7 us
    all_gather x1, blocking collectives, local(): lax.all_gather(w_hot_gu, 'expert', axis=2, tiled=True)  38.7 us
    all_to_all x1, waiting for transfers between devices, local(): lax.all_to_all(send_s, 'expert', split_axis=0, concat_axis=0, tiled=True)  37.2 us
    all_gather x1, blocking collectives, local(): lax.all_gather(hot_x, 'dp', axis=0, tiled=True)  33.8 us
  transfers between devices with their start and end apart: 11, of which 6 were waited for; matrix products, arithmetic and copies ran while one was open for 12% of the time, Pallas kernels for 0%

commit v1 on v0

v1 whole, which is shorter than its diff:
```python
import functools

import jax
import jax.numpy as jnp
import numpy as np
from jax import lax
from jax.experimental import pallas as pl
from jax.experimental.pallas import tpu as pltpu
from jax.sharding import PartitionSpec as P

MESH = pl.DeviceIdType.MESH
BF = jnp.bfloat16
F32 = jnp.float32
CAP = 6
MSG = 16
NZ, NX, NY = 8, 4, 4


def dot(a, b):
    return jnp.dot(a, b, preferred_element_type=F32)


def dot_nt(a, b):
    return lax.dot_general(a, b, (((1,), (1,)), ((), ())), preferred_element_type=F32)


def hit(a, b):
    return jnp.where(a == b, 1.0, 0.0).astype(BF)


def iota(shape, axis):
    return lax.broadcasted_iota(jnp.int32, shape, axis)


class Sems:
    def __init__(self, send, recv):
        self.send, self.recv, self.ids = send, recv, {}

    def __call__(self, name):
        if name not in self.ids:
            self.ids[name] = len(self.ids)
        n = self.ids[name]
        return self.send.at[n], self.recv.at[n]


def kernel(
    tok, cot, routes_row, routes_col, gates, hidx_row, hidx_col, hgate, perm_col, perm_row,
    wgu_in, wdn_in, hw_in,
    lo_out, ig_out, ggu_out, gdn_out, ghw_out,
    wgu, wdn, hxs, hw, msend, mrecv, mback, rxs, xt, ht, hid, dact,
    pgu, pdn, phb, qgu, qdn, qhb, rgu, rdn, rhb, hown, hg, hgr, hgz,
    sem_s, sem_r, a_s, a_r, b_s, b_r, loc,
):
    me, e = lax.axis_index("dp"), lax.axis_index("expert")
    y, c = me // 2, me % 2
    z, x = e // NX, e % NX
    yp, ym, y2 = (y + 1) % NY, (y + 3) % NY, (y + 2) % NY
    xp, xm, x2 = (x + 1) % NX, (x + 3) % NX, (x + 2) % NX
    up, down, mate = (2 * yp + c, e), (2 * ym + c, e), (2 * y + 1 - c, e)
    right, left = (me, NX * z + xp), (me, NX * z + xm)
    sems = Sems(sem_s, sem_r)
    started = []

    def send(name, src, dst, dev):
        s, r = sems(name)
        copy = pltpu.make_async_remote_copy(
            src_ref=src, dst_ref=dst, send_sem=s, recv_sem=r, device_id=dev, device_id_type=MESH
        )
        copy.start()
        started.append(copy)

    def arrived(name, dst):
        s, r = sems(name)
        pltpu.make_async_remote_copy(
            src_ref=dst, dst_ref=dst, send_sem=s, recv_sem=r, device_id=mate, device_id_type=MESH
        ).wait_recv()

    barrier = pltpu.get_barrier_semaphore()
    for dev in (up, down, mate):
        pl.semaphore_signal(barrier, inc=1, device_id=dev, device_id_type=MESH)

    @pl.loop(1, NZ * NX)
    def _(j):
        pl.semaphore_signal(
            barrier, inc=1, device_id=(me, (e + j) % (NZ * NX)), device_id_type=MESH
        )

    own_gu = pltpu.make_async_copy(wgu_in.at[0], wgu.at[me], loc.at[0])
    own_dn = pltpu.make_async_copy(wdn_in.at[0], wdn.at[me], loc.at[1])
    own_gu.start()
    own_dn.start()

    n_tok, width = tok.shape
    third = 3 * width // 4 // 3
    n_hot = hidx_col.shape[0]
    pick_hot = hit(iota((n_hot, n_tok), 1), hidx_col[...])
    hown[0:n_hot] = dot(pick_hot, tok[...]).astype(BF)
    hown[n_hot:] = (hgate[...] * dot(pick_hot, cot[...])).astype(BF)
    hxs[me] = hown[...]
    hw[z, x] = hw_in[...]

    rr, rc = routes_row[...], routes_col[...]
    onehot = hit(iota((NZ * NX, n_tok), 0), rr)
    ahead = jnp.where(iota((n_tok, n_tok), 0) < iota((n_tok, n_tok), 1), 1.0, 0.0).astype(BF)
    pos_r = jnp.sum(dot(onehot, ahead) * onehot.astype(F32), axis=0, keepdims=True).astype(jnp.int32)
    onehot = hit(iota((n_tok, n_tok), 1), rc)
    ahead = jnp.where(iota((n_tok, n_tok), 1) < iota((n_tok, n_tok), 0), 1.0, 0.0).astype(BF)
    pos_c = jnp.sum(dot(ahead, onehot) * onehot.astype(F32), axis=1, keepdims=True).astype(jnp.int32)

    def tail_code(route, pos, i):
        high = jnp.where(pos >= 3, 1, 0)
        return jnp.where(pos - 3 * high == i, route * MSG + 12 + high, -9)

    rows = NZ * NX * MSG
    q_id = iota((rows, n_tok), 0)
    main_x = hit(q_id, rr * MSG + pos_r)
    main_s = hit(q_id, rr * MSG + pos_r + CAP)

    def columns(k, size):
        part = slice(k, k + size)
        return tok[:, part], (gates[...] * cot[:, part].astype(F32)).astype(BF)

    tail_x, tail_s = columns(3 * third, third)
    for i in range(3):
        code = tail_code(rr, pos_r, i)
        choose = jnp.concatenate([main_x, main_s, hit(q_id, code), hit(q_id, code + 2)], axis=1)
        part_x, part_s = columns(i * third, third)
        data = jnp.concatenate([part_x, part_s, tail_x, tail_s], axis=0)
        msend[:, :, i * third : (i + 1) * third] = (
            dot(choose, data).astype(BF).reshape(NZ * NX, MSG, third)
        )
    mrecv[e] = msend[e]

    pl.semaphore_wait(barrier, NZ * NX + 2)

    halves = {
        "h": (hown, hxs, hxs.shape[1] // 2),
        "g": (wgu_in.at[0], wgu, wgu.shape[1] // 2),
        "d": (wdn_in.at[0], wdn, wdn.shape[1] // 2),
    }

    def half(name, block, k):
        size = halves[name][2]
        return halves[name][1].at[block, pl.ds(k * size, size)]

    def own_half(name, k):
        size = halves[name][2]
        return halves[name][0].at[pl.ds(k * size, size)]

    def ring_start(names):
        for k in (0, 1):
            for name in names:
                send((name, "up", k), own_half(name, k), half(name, me, k), up)
                send((name, "down", 1 - k), own_half(name, 1 - k), half(name, me, 1 - k), down)
        for name in names:
            send((name, "mate"), halves[name][0], halves[name][1].at[me], mate)

    def ring_near(names, k):
        for name in names:
            low, high = half(name, 2 * ym + c, k), half(name, 2 * yp + c, 1 - k)
            arrived((name, "up", k), low)
            if k == 0:
                send((name, "up", 2), low, low, up)
            send((name, "mate", 0, k), low, low, mate)
            arrived((name, "down", 1 - k), high)
            if k == 0:
                send((name, "down", 2), high, high, down)
            send((name, "mate", 1, k), high, high, mate)

    def ring_far(names):
        for name in names:
            low, high = half(name, 2 * y2 + c, 0), half(name, 2 * y2 + c, 1)
            arrived((name, "up", 2), low)
            send((name, "mate", 2, 0), low, low, mate)
            arrived((name, "down", 2), high)
            send((name, "mate", 2, 1), high, high, mate)

    def ring_end(names):
        d = 1 - c
        for name in names:
            arrived((name, "mate"), halves[name][1].at[2 * y + d])
            for k in (0, 1):
                arrived((name, "mate", 0, k), half(name, 2 * ym + d, k))
                arrived((name, "mate", 1, k), half(name, 2 * yp + d, 1 - k))
                arrived((name, "mate", 2, k), half(name, 2 * y2 + d, k))

    ring_start(["h"])
    for j in range(1, NZ):
        send(("hz", j), hw_in, hw.at[z, x], (me, NX * ((z + j) % NZ) + x))

    def token_copy(j, sign, out_ref, in_ref, s, r):
        peer = (e + j) % (NZ * NX) if sign else (e + NZ * NX - j) % (NZ * NX)
        return pltpu.make_async_remote_copy(
            src_ref=out_ref.at[peer] if sign else in_ref.at[peer],
            dst_ref=in_ref.at[e] if sign else in_ref.at[peer],
            send_sem=s.at[j],
            recv_sem=r.at[j],
            device_id=(me, peer),
            device_id_type=MESH,
        )

    ring_start(["g", "d"])

    @pl.loop(1, NZ * NX)
    def _(j):
        token_copy(j, True, msend, mrecv, a_s, a_r).start()

    ring_near(["h"], 0)
    ring_near(["h"], 1)

    for j in range(1, NZ):
        arrived(("hz", j), hw.at[(z + NZ - j) % NZ, x])

    def hw_half(col, k):
        return hw.at[pl.ds(k * (NZ // 2), NZ // 2), col]

    for k in (0, 1):
        send(("x", "right", k), hw_half(x, k), hw_half(x, k), right)
        send(("x", "left", 1 - k), hw_half(x, 1 - k), hw_half(x, 1 - k), left)
    ring_far(["h"])
    ring_near(["g", "d"], 0)
    arrived(("x", "right", 0), hw_half(xm, 0))
    send(("x", "right", 2), hw_half(xm, 0), hw_half(xm, 0), right)
    arrived(("x", "left", 1), hw_half(xp, 1))
    send(("x", "left", 2), hw_half(xp, 1), hw_half(xp, 1), left)
    arrived(("x", "right", 1), hw_half(xm, 1))
    arrived(("x", "left", 0), hw_half(xp, 0))
    arrived(("x", "right", 2), hw_half(x2, 0))
    arrived(("x", "left", 2), hw_half(x2, 1))
    ring_end(["h"])
    own_gu.wait()
    own_dn.wait()

    n_dp = hxs.shape[0]
    n_all = n_dp * n_hot
    hot_x = hxs[:, 0:n_hot, :].reshape(n_all, width)
    hot_s = hxs[:, n_hot:, :].reshape(n_all, width)
    act = dot(hot_x, hw[:, :, :, 0:256].reshape(width, 256))
    hot_g, hot_u = act[:, 0:128], act[:, 128:256]
    hot_dh = dot(hot_s, hw[:, :, :, 256:384].reshape(width, 128))
    sigma = 1.0 / (1.0 + jnp.exp(-hot_g))
    hot_h = (hot_g * sigma * hot_u).astype(BF)
    hot_d = jnp.concatenate(
        [
            (hot_dh * hot_u * sigma * (1.0 + hot_g * (1.0 - sigma))).astype(BF),
            (hot_dh * hot_g * sigma).astype(BF),
        ],
        axis=1,
    )
    quarter = width // 4
    for k in range(4):
        part = slice(k * quarter, (k + 1) * quarter)
        zs = slice(2 * k, 2 * k + 2)
        w_gu = hw[zs, :, :, 0:256].reshape(quarter, 256)
        w_dn = hw[zs, :, :, 256:384].reshape(quarter, 128)
        phb[:, 0:n_hot, part] = dot_nt(hot_h, w_dn).astype(BF).reshape(n_dp, n_hot, quarter)
        phb[:, n_hot:, part] = dot_nt(hot_d, w_gu).astype(BF).reshape(n_dp, n_hot, quarter)
        x_t = hxs[:, 0:n_hot, part].reshape(n_all, quarter).T
        s_t = hxs[:, n_hot:, part].reshape(n_all, quarter).T
        block = (2, NX, hw.shape[2])
        hg[zs, :, :, 0:256] = dot(x_t, hot_d).astype(BF).reshape(*block, 256)
        hg[zs, :, :, 256:384] = dot(s_t, hot_h).astype(BF).reshape(*block, 128)

    sums = {
        "h": (phb, qhb, rhb, hxs.shape[1] // 2, 32),
        "g": (pgu, qgu, rgu, wgu.shape[1] // 2, 32),
        "d": (pdn, qdn, rdn, wdn.shape[1] // 2, 48),
    }

    def chip_send(name, yy):
        p, q = sums[name][0:2]
        send((name, "chip", (yy,)), p.at[2 * CHIP[yy] + 1 - c], q.at[CHIP[yy]], mate)

    CHIP = {"y": y, "p": yp, "m": ym, "2": y2}

    def chip_add(name, yy):
        p, q, _, size, step = sums[name]
        arrived((name, "chip", (yy,)), q.at[CHIP[yy]])

        @pl.loop(0, 2 * size // step)
        def _(i):
            part = pl.ds(pl.multiple_of(i * step, step), step)
            q[CHIP[yy], part] = (
                q[CHIP[yy], part].astype(F32) + p[2 * CHIP[yy] + c, part].astype(F32)
            ).astype(BF)

    def q_half(name, yy, k):
        size = sums[name][3]
        return sums[name][1].at[CHIP[yy], pl.ds(k * size, size)]

    def r_half(name, slot, k):
        size = sums[name][3]
        return sums[name][2].at[slot, pl.ds(k * size, size)]

    def far_send(name):
        send((name, "far", 0), q_half(name, "2", 0), r_half(name, 0, 0), up)
        send((name, "far", 1), q_half(name, "2", 1), r_half(name, 0, 1), down)

    def near_send(name, first):
        if first:
            send((name, "sum", 0), q_half(name, "p", 1), r_half(name, 1, 1), up)
            send((name, "sum", 1), q_half(name, "m", 0), r_half(name, 2, 0), down)
        else:
            send((name, "sum", 2), q_half(name, "p", 0), r_half(name, 1, 0), up)
            send((name, "sum", 3), q_half(name, "m", 1), r_half(name, 2, 1), down)

    def near_add(name):
        _, q, r, size, step = sums[name]
        step = min(step, size)
        for k, yy in ((0, "p"), (1, "m")):
            arrived((name, "far", k), r_half(name, 0, k))

            @pl.loop(0, size // step)
            def _(i):
                part = pl.ds(pl.multiple_of(k * size + i * step, 16), step)
                q[CHIP[yy], part] = (
                    q[CHIP[yy], part].astype(F32) + r[0, part].astype(F32)
                ).astype(BF)

    def sum_wait(name):
        arrived((name, "sum", 0), r_half(name, 1, 1))
        arrived((name, "sum", 1), r_half(name, 2, 0))
        arrived((name, "sum", 2), r_half(name, 1, 0))
        arrived((name, "sum", 3), r_half(name, 2, 1))

    for yy in "2pmy":
        chip_send("h", yy)

    def hg_half(col, k):
        return hg.at[pl.ds(k * (NZ // 2), NZ // 2), col]

    def hgr_half(slot, k):
        return hgr.at[slot, pl.ds(k * (NZ // 2), NZ // 2)]

    send(("gx", "far", 0), hg_half(x2, 0), hgr_half(0, 0), right)
    send(("gx", "far", 1), hg_half(x2, 1), hgr_half(0, 1), left)
    send(("gx", "sum", 0), hg_half(xp, 1), hgr_half(1, 1), right)
    send(("gx", "sum", 1), hg_half(xm, 0), hgr_half(2, 0), left)

    ring_near(["g", "d"], 1)
    for yy in "2pmy":
        chip_add("h", yy)
    far_send("h")
    near_send("h", True)

    @pl.loop(1, NZ * NX)
    def _(j):
        token_copy(j, False, msend, mrecv, a_s, a_r).wait_recv()

    n_row = rxs.shape[0] // 2
    col_id = iota((2 * n_row, rows), 1)
    straight = hit(col_id, perm_col[:, 0:1])
    tail = None
    for i in range(3):
        part = mrecv[:, :, i * third : (i + 1) * third].reshape(rows, third)
        rxs[:, i * third : (i + 1) * third] = dot(straight, part).astype(BF)
        piece = dot(hit(col_id, perm_col[:, i + 1 : i + 2]), part)
        tail = piece if tail is None else tail + piece
    rxs[:, 3 * third :] = tail.astype(BF)
    for k in range(4):
        part = slice(k * third, (k + 1) * third)
        xt[part] = rxs[0:n_row, part].T

    arrived(("gx", "far", 0), hgr_half(0, 0))
    arrived(("gx", "far", 1), hgr_half(0, 1))
    for k, col in ((0, xp), (1, xm)):
        for i in range(NZ // 2):
            n = k * (NZ // 2) + i
            hg[n, col] = (hg[n, col].astype(F32) + hgr[0, n].astype(F32)).astype(BF)
    send(("gx", "sum", 2), hg_half(xp, 0), hgr_half(1, 0), right)
    send(("gx", "sum", 3), hg_half(xm, 1), hgr_half(2, 1), left)

    ring_far(["g", "d"])
    arrived(("gx", "sum", 0), hgr_half(1, 1))
    arrived(("gx", "sum", 1), hgr_half(2, 0))
    arrived(("gx", "sum", 2), hgr_half(1, 0))
    arrived(("gx", "sum", 3), hgr_half(2, 1))
    for n in range(NZ):
        hg[n, x] = (
            hg[n, x].astype(F32) + hgr[1, n].astype(F32) + hgr[2, n].astype(F32)
        ).astype(BF)
    hgz[z] = hg[z, x]
    for j in range(1, NZ):
        there = (z + j) % NZ
        send(("gz", j), hg.at[there, x], hgz.at[z], (me, NX * there + x))
    near_add("h")
    near_send("h", False)
    ring_end(["g", "d"])

    hidden = wdn.shape[0] * wdn.shape[1]
    model = wgu.shape[0] * wgu.shape[1]
    w_dn2 = wdn.reshape(hidden, width)

    @pl.loop(0, hidden // 256)
    def _(n):
        first = pl.ds(pl.multiple_of(n * 256, 256), 256)
        second = pl.ds(pl.multiple_of(hidden + n * 256, 256), 256)
        g = dot(rxs[0:n_row], wgu[:, :, first].reshape(model, 256))
        u = dot(rxs[0:n_row], wgu[:, :, second].reshape(model, 256))
        dh = dot_nt(rxs[n_row:], w_dn2[first])
        s = 1.0 / (1.0 + jnp.exp(-g))
        h = (g * s * u).astype(BF)
        hid[:, first] = h
        ht[first] = h.T
        dact[:, first] = (dh * u * s * (1.0 + g * (1.0 - s))).astype(BF)
        dact[:, second] = (dh * g * s).astype(BF)

    half_rows = wgu.shape[1]

    def grad_gu(yy):
        lhs = xt[pl.ds(pl.multiple_of(CHIP[yy] * 2 * half_rows, 16), 2 * half_rows)]

        @pl.loop(0, 2 * hidden // 256)
        def _(n):
            part = pl.ds(pl.multiple_of(n * 256, 256), 256)
            both = dot(lhs, dact[:, part]).astype(BF)
            pgu[pl.ds(2 * CHIP[yy], 2), :, part] = both.reshape(2, half_rows, 256)

        chip_send("g", yy)

    grad_gu("2")

    @pl.loop(0, width // 256)
    def _(n):
        part = pl.ds(pl.multiple_of(n * 256, 256), 256)
        pdn[:, :, part] = dot(ht[...], rxs[n_row:, part]).astype(BF).reshape(*pdn.shape[0:2], 256)

    for yy in "2pmy":
        chip_send("d", yy)
    for name in "gd":
        chip_add(name, "2")
        far_send(name)

    @pl.loop(0, width // 256)
    def _(n):
        part = pl.ds(pl.multiple_of(n * 256, 256), 256)
        rxs[0:n_row, part] = dot(hid[...], w_dn2[:, part]).astype(BF)

    for k in range(wgu.shape[0] // 2):
        w = wgu[2 * k : 2 * k + 2].reshape(2 * half_rows, 2 * hidden)
        rxs[n_row:, k * 2 * half_rows : (k + 1) * 2 * half_rows] = dot_nt(dact[...], w).astype(BF)

    @pl.loop(1, NZ * NX)
    def _(j):
        token_copy(j, True, msend, mrecv, a_s, a_r).wait_send()

    row_id = iota((rows, 2 * n_row), 0)
    straight = hit(row_id, perm_row[0:1])
    for i in range(3):
        part = slice(i * third, (i + 1) * third)
        mixed = dot(straight, rxs[:, part]) + dot(
            hit(row_id, perm_row[i + 1 : i + 2]), rxs[:, 3 * third :]
        )
        msend[:, :, part] = mixed.astype(BF).reshape(NZ * NX, MSG, third)
    mback[e] = msend[e]

    @pl.loop(1, NZ * NX)
    def _(j):
        token_copy(j, True, msend, mback, b_s, b_r).start()

    grad_gu("p")
    grad_gu("m")
    for yy in "pm":
        for name in "gd":
            chip_add(name, yy)
    for name in "gd":
        near_send(name, True)
    grad_gu("y")
    for name in "gd":
        near_add(name)
        near_send(name, False)
    for name in "gd":
        chip_add(name, "y")

    total = hgz[z].astype(F32)
    for j in range(1, NZ):
        there = (z + NZ - j) % NZ
        arrived(("gz", j), hgz.at[there])
        total = total + hgz[there].astype(F32)
    scale = 1.0 / 32.0
    ghw_out[...] = (total * scale).astype(BF)

    sum_wait("h")
    hot_sum = qhb[y].astype(F32) + rhb[1].astype(F32) + rhb[2].astype(F32)
    back = jnp.concatenate([hgate[...] * hot_sum[0:n_hot], hot_sum[n_hot:]], axis=1)
    upper = back.astype(BF)
    back = jnp.concatenate([upper, (back - upper.astype(F32)).astype(BF)], axis=0)
    spread = hit(iota((n_tok, 2 * n_hot), 0), hidx_row[...])

    @pl.loop(1, NZ * NX)
    def _(j):
        token_copy(j, False, msend, mback, b_s, b_r).wait_recv()

    lane_id = iota((n_tok, rows), 1)
    code = rc * MSG + pos_c
    straight = jnp.concatenate([hit(lane_id, code), hit(lane_id, code + CAP)], axis=0)
    tail = None
    for i in range(4):
        part = slice(i * third, (i + 1) * third)
        if i < 3:
            data = mback[:, :, part].reshape(rows, third)
            got = dot(straight, data)
            code = tail_code(rc, pos_c, i)
            piece = dot(
                jnp.concatenate([hit(lane_id, code), hit(lane_id, code + 2)], axis=0), data
            )
            tail = piece if tail is None else tail + piece
        else:
            got = tail
        hot_part = dot(spread, back[:, part])
        hot_grad = dot(spread, back[:, width + i * third : width + (i + 1) * third])
        lo_out[:, part] = (gates[...] * got[0:n_tok] + hot_part).astype(BF)
        ig_out[:, part] = (got[n_tok:] + hot_grad).astype(BF)

    for name, out in (("g", ggu_out), ("d", gdn_out)):
        _, q, r, size, step = sums[name]
        sum_wait(name)

        @pl.loop(0, 2 * size // step)
        def _(i):
            part = pl.ds(pl.multiple_of(i * step, step), step)
            value = q[y, part].astype(F32) + r[1, part].astype(F32) + r[2, part].astype(F32)
            out[0, part] = (value * scale).astype(BF)

    for copy in started:
        copy.wait_send()

    @pl.loop(1, NZ * NX)
    def _(j):
        token_copy(j, True, msend, mback, b_s, b_r).wait_send()


def row_tables(n_expert, n_row):
    table = np.full((4, 2 * n_row), -1, np.int32)
    for k in range(2):
        for p in range(n_expert):
            for r in range(CAP):
                n = k * n_row + p * CAP + r
                table[0, n] = p * MSG + k * CAP + r
                place = k * CAP + r
                table[1 + place % 3, n] = p * MSG + 12 + place // 3
    return table


def local(
    tokens, cotangent, routes, gates, hot_index, hot_gate, w_gate_up, w_down, w_hot_gu, w_hot_dn
):
    n_dp, n_e = lax.axis_size("dp"), lax.axis_size("expert")
    n_tok, width = tokens.shape
    n_hot = hot_index.shape[0]
    rows_gu, double = w_gate_up.shape[1:]
    rows_dn = w_down.shape[1]
    units, features = w_hot_dn.shape
    n_row = 256
    table = row_tables(n_e, n_row)
    perm_row = jnp.asarray(np.concatenate([table, np.full_like(table, -1)], axis=0))
    perm_col = jnp.asarray(np.pad(table.T, ((0, 0), (0, 124)), constant_values=-1))
    hot_w = jnp.concatenate([w_hot_gu, w_hot_dn[None]], axis=0)
    hot_w = jnp.pad(hot_w, ((0, 0), (0, 128 - units), (0, 0))).transpose(2, 0, 1)
    hot_w = hot_w.reshape(features, 384)
    vmem = pl.BlockSpec(memory_space=pltpu.VMEM)
    any_space = pl.BlockSpec(memory_space=pl.ANY)
    msg = (n_e, MSG, 3 * width // 4)
    hot2 = 2 * n_hot
    dma = pltpu.SemaphoreType.DMA
    outs = pl.pallas_call(
        kernel,
        out_shape=(
            jax.ShapeDtypeStruct((n_tok, width), BF),
            jax.ShapeDtypeStruct((n_tok, width), BF),
            jax.ShapeDtypeStruct(w_gate_up.shape, BF),
            jax.ShapeDtypeStruct(w_down.shape, BF),
            jax.ShapeDtypeStruct(hot_w.shape, BF),
        ),
        in_specs=[vmem] * 10 + [any_space] * 2 + [vmem],
        out_specs=(vmem,) * 5,
        scratch_shapes=[
            pltpu.VMEM((n_dp, rows_gu, double), BF),
            pltpu.VMEM((n_dp, rows_dn, width), BF),
            pltpu.VMEM((n_dp, hot2, width), BF),
            pltpu.VMEM((NZ, NX, features, 384), BF),
            pltpu.VMEM(msg, BF),
            pltpu.VMEM(msg, BF),
            pltpu.VMEM(msg, BF),
            pltpu.VMEM((2 * n_row, width), BF),
            pltpu.VMEM((width, n_row), BF),
            pltpu.VMEM((double // 2, n_row), BF),
            pltpu.VMEM((n_row, double // 2), BF),
            pltpu.VMEM((n_row, double), BF),
            pltpu.VMEM((n_dp, rows_gu, double), BF),
            pltpu.VMEM((n_dp, rows_dn, width), BF),
            pltpu.VMEM((n_dp, hot2, width), BF),
            pltpu.VMEM((NY, rows_gu, double), BF),
            pltpu.VMEM((NY, rows_dn, width), BF),
            pltpu.VMEM((NY, hot2, width), BF),
            pltpu.VMEM((3, rows_gu, double), BF),
            pltpu.VMEM((3, rows_dn, width), BF),
            pltpu.VMEM((3, hot2, width), BF),
            pltpu.VMEM((hot2, width), BF),
            pltpu.VMEM((NZ, NX, features, 384), BF),
            pltpu.VMEM((3, NZ, features, 384), BF),
            pltpu.VMEM((NZ, features, 384), BF),
            dma((112,)),
            dma((112,)),
            dma((n_e,)),
            dma((n_e,)),
            dma((n_e,)),
            dma((n_e,)),
            dma((2,)),
        ],
        compiler_params=pltpu.CompilerParams(
            collective_id=0, has_side_effects=True, vmem_limit_bytes=67043328
        ),
        name="expert_layer",
    )(
        tokens, cotangent, routes.reshape(1, n_tok), routes, gates,
        jnp.tile(hot_index, 2).reshape(1, hot2), hot_index.reshape(n_hot, 1),
        hot_gate.reshape(n_hot, 1), perm_col, perm_row, w_gate_up, w_down, hot_w,
    )
    layer_out, input_grad, grad_gu, grad_dn, grad_hot = outs
    grad_hot = grad_hot.reshape(features, 3, 128)[:, :, :units].transpose(1, 2, 0)
    return layer_out, input_grad, grad_gu, grad_dn, grad_hot[0:2], grad_hot[2]


def solution(mesh):
    placed = (
        P(("dp", "expert"), None),
        P(("dp", "expert"), None),
        P(("dp", "expert"), None),
        P(("dp", "expert"), None),
        P(("dp", "expert")),
        P(("dp", "expert")),
        P("expert", "dp", None),
        P("expert", "dp", None),
        P(None, "dp", "expert"),
        P("dp", "expert"),
    )
    return jax.shard_map(
        local,
        mesh=mesh,
        in_specs=placed,
        out_specs=(
            P(("dp", "expert"), None),
            P(("dp", "expert"), None),
            P("expert", "dp", None),
            P("expert", "dp", None),
            P(None, "dp", "expert"),
            P("dp", "expert"),
        ),
        check_vma=False,
    )
```

time: 536 us -> 172 us (0.32)
  waiting for transfers between devices: 275 us -> 0 us
  Pallas kernels: 0 us -> 156 us
  blocking collectives: 148 us -> 0 us
  starting transfers between devices: 32.1 us -> 0 us
  matrix products: 31.6 us -> 0 us
  between operations: 16.6 us -> 0.69 us
  local copies, waits for them, and re-layouts: 22.6 us -> 13.4 us
  other arithmetic: 8.81 us -> 1.44 us
    reduce_scatter x4 -> x0, waiting for transfers between devices: 168 us -> none  [the longest x1 66.3 us: local(): lax.psum_scatter(part_hot_dn.astype(jnp.bfloat16), 'expert', scatter_dime...]
    pallas_call x0 -> x1, Pallas kernels: none -> 156 us  [local(): pl.pallas_call(kernel, out_shape=(jax.ShapeDtypeStruct((n_tok, width), BF...]
    all_gather x4 -> x0, blocking collectives: 148 us -> none  [the longest x1 61.8 us: local(): lax.all_gather(w_hot_dn, 'expert', axis=1, tiled=True)]
    all_to_all x4 -> x0, waiting for transfers between devices: 64.9 us -> none  [the longest x1 37.2 us: local(): lax.all_to_all(send_s, 'expert', split_axis=0, concat_axis=0, tiled=True)]
    unnamed x8 -> x0, waiting for transfers between devices: 41.7 us -> none
    all_to_all x4 -> x0, starting transfers between devices: 31.6 us -> none  [the longest x1 11.2 us: local(): lax.all_to_all(send_x, 'expert', split_axis=0, concat_axis=0, tiled=True)]
    dot_general x15 -> x0, matrix products: 31.6 us -> none  [the longest x1 6.04 us: expert_forward(): act = jnp.dot(rows_x, w_gu, preferred_element_type=jnp.float32)]
    reshape x8 -> x3, local copies, waits for them, and re-layouts: 9.47 us -> 3.51 us  [the longest x1 1.33 us: local(): hot_gate.reshape(n_hot, 1)]
  transfers between devices with their start and end apart: 11 -> 0, of which waited for: 6 -> 0; matrix products, arithmetic and copies ran while one was open for 12% -> 0% of each run, Pallas kernels for 0% -> 0%
where the time goes in v1:
time: 172 us; the launch traced here: 171 us
  Pallas kernels  156 us (91%)
  local copies, waits for them, and re-layouts  13.4 us (8%)
    pallas_call x1, Pallas kernels, local(): pl.pallas_call(kernel, out_shape=(jax.ShapeDtypeStruct((n_tok, width), BF...  156 us
    unnamed x22, local copies, waits for them, and re-layouts  8.33 us

profile of v1, /device:TPU:7, one launch (start us, length us, event | category | flops | bytes accessed | tf_op | source)
XLA Modules:
  0.0 171.5 jit_solution(11041396651272571244)
XLA Ops:
  0.6 0.0 copy-start.4
  0.6 0.7 tile.2
  1.3 0.6 reshape_tile.3.hidx_row
  1.9 1.3 copy.34.hgate
  3.2 1.3 copy.33.hidx_col
  4.6 0.0 copy-done.4
  4.6 0.0 copy-start.6
  4.6 1.4 copy_bitcast_fusion.hw_in
  6.0 0.0 copy-done.6
  6.0 0.0 copy-start.5
  6.0 0.7 copy.32.gates
  6.7 0.0 copy-done.5
  6.7 0.7 copy.31.routes_col
  7.5 156.0 %expert_layer.1 = (bf16[128,2560]{1,0:T(8,128)(2,1)}, bf16[128,2560]{1,0:T(8,128)(2,1)}, bf16[1,320,1536]{2,1,0:T(8,128)(2,1)}, bf16[1,96,2560]{2,1,0:T(8,128)(2,1)}, bf16[80,384]{1,0:T(8,128)(2,1)}) custom-call(bf16[128,2560]{1,0:T(8,128)(2,1)} %tok.1, bf16[128,2560]{1,0:T(8,128)(2,1)} %cot.1, s32[1,128]{1,0:T(1,128)} %bitcast.17, ...), custom_call_target="tpu_custom_call" | custom-call | tf_op jit(solution)/shard_map/expert_layer/pallas_call | solution.py:566
  163.5 0.9 reshape.32
  164.4 0.0 copy-start.3
  164.4 0.6 copy-done.3
  165.0 0.0 slice-start
  165.0 0.6 copy.40
  165.6 0.2 slice-done
  165.8 0.0 copy-start.1
  165.8 0.6 copy.35
  166.4 0.0 copy-start
  166.4 2.0 %copy.45 = bf16[128,2560]{1,0:T(8,128)(2,1)} copy(bf16[128,2560]{1,0:T(8,128)(2,1)} %get-tuple-element.34) | data formatting | bytes 1310720
  168.5 0.0 copy-done.1
  168.5 0.8 copy.46
  169.3 0.0 copy-done
  169.3 0.0 copy-start.2
  169.3 0.9 copy.47
  170.3 0.4 copy-done.2
  170.7 0.8 copy.48
  (2 shorter events, 0.1 us)
Async XLA Ops:
  0.6 3.9 %copy-start.4 = (bf16[96,80]{0,1:T(8,128)(2,1)S(1)}, bf16[96,80]{0,1:T(8,128)(2,1)}, u32[]{:S(2)}) copy-start(bf16[96,80]{0,1:T(8,128)(2,1)} %param.21) | copy-start | bytes 46084
  4.6 1.4 copy-start.6
  6.0 0.7 copy-start.5
  164.4 0.6 copy-start.3
  165.0 0.8 slice-start
  165.8 2.7 %copy-start.1 = (bf16[128,2560]{1,0:T(8,128)(2,1)S(1)}, bf16[128,2560]{1,0:T(8,128)(2,1)}, u32[]{:S(2)}) copy-start(bf16[128,2560]{1,0:T(8,128)(2,1)} %get-tuple-element.35) | copy-start | bytes 1966084
  166.4 2.9 %copy-start = (bf16[1,320,1536]{2,1,0:T(8,128)(2,1)S(1)}, bf16[1,320,1536]{2,1,0:T(8,128)(2,1)}, u32[]{:S(2)}) copy-start(bf16[1,320,1536]{2,1,0:T(8,128)(2,1)} %get-tuple-element.36) | copy-start | bytes 2949124
  169.3 1.4 copy-start.2

commit v2 on v1

--- a/solution.py
+++ b/solution.py
@@ -2,7 +2,6 @@
 
 import jax
 import jax.numpy as jnp
-import numpy as np
 from jax import lax
 from jax.experimental import pallas as pl
 from jax.experimental.pallas import tpu as pltpu
@@ -12,7 +11,7 @@
 BF = jnp.bfloat16
 F32 = jnp.float32
 CAP = 6
-MSG = 16
+MSG = 8
 NZ, NX, NY = 8, 4, 4
 
 
@@ -44,12 +43,13 @@
 
 
 def kernel(
-    tok, cot, routes_row, routes_col, gates, hidx_row, hidx_col, hgate, perm_col, perm_row,
-    wgu_in, wdn_in, hw_in,
-    lo_out, ig_out, ggu_out, gdn_out, ghw_out,
-    wgu, wdn, hxs, hw, msend, mrecv, mback, rxs, xt, ht, hid, dact,
+    tok_in, cot_in, wgu_in, wdn_in,
+    routes_row, gates_row, hidx_row, hgate_row, hot_gu_in, hot_dn_in,
+    lo_out, ig_out, ggu_out, gdn_out, ghg_out, ghd_out,
+    tok, cot, hw_in, lo_buf, ig_buf, ghg_buf, gates, hgate,
+    wgu, wdn, hxs, hw, send_x, send_s, recv_x, recv_s, back_o, back_g, rx, rs, xt, ht, hid, dact, acc, dh_acc,
     pgu, pdn, phb, qgu, qdn, qhb, rgu, rdn, rhb, hown, hg, hgr, hgz,
-    sem_s, sem_r, a_s, a_r, b_s, b_r, loc,
+    sem_s, sem_r, x_s, x_r, s_s, s_r, o_s, o_r, g_s, g_r, loc,
 ):
     me, e = lax.axis_index("dp"), lax.axis_index("expert")
     y, c = me // 2, me % 2
@@ -85,21 +85,43 @@
             barrier, inc=1, device_id=(me, (e + j) % (NZ * NX)), device_id_type=MESH
         )
 
-    own_gu = pltpu.make_async_copy(wgu_in.at[0], wgu.at[me], loc.at[0])
-    own_dn = pltpu.make_async_copy(wdn_in.at[0], wdn.at[me], loc.at[1])
-    own_gu.start()
-    own_dn.start()
+    def fetch(n, src, dst):
+        copy = pltpu.make_async_copy(src, dst, loc.at[n])
+        copy.start()
+        return copy
+
+    rows_in = (fetch(0, tok_in, tok), fetch(1, cot_in, cot))
+    later_in = (
+        fetch(2, wgu_in.at[0], wgu.at[me]),
+        fetch(3, wdn_in.at[0], wdn.at[me]),
+    )
 
     n_tok, width = tok.shape
     third = 3 * width // 4 // 3
-    n_hot = hidx_col.shape[0]
-    pick_hot = hit(iota((n_hot, n_tok), 1), hidx_col[...])
+    n_hot = hidx_row.shape[1]
+
+    def turned(row):
+        n = row.shape[1]
+        return jnp.sum(jnp.where(iota((n, n), 0) == iota((n, n), 1), row, 0.0), axis=1, keepdims=True)
+
+    rr = routes_row[...]
+    rc = turned(rr.astype(F32)).astype(jnp.int32)
+    gates[...] = turned(gates_row[...])
+    hgate[...] = turned(hgate_row[...])
+    hidx_col = turned(hidx_row[...].astype(F32)).astype(jnp.int32)
+    units = hot_dn_in.shape[1]
+    zeros = jnp.zeros((hw_in.shape[0], 128 - units), BF)
+    for n, w in enumerate((hot_gu_in[0], hot_gu_in[1], hot_dn_in[...])):
+        hw_in[:, n * 128 : (n + 1) * 128] = jnp.concatenate([w, zeros], axis=1)
+
+    for copy in rows_in:
+        copy.wait()
+    pick_hot = hit(iota((n_hot, n_tok), 1), hidx_col)
     hown[0:n_hot] = dot(pick_hot, tok[...]).astype(BF)
     hown[n_hot:] = (hgate[...] * dot(pick_hot, cot[...])).astype(BF)
     hxs[me] = hown[...]
     hw[z, x] = hw_in[...]
 
-    rr, rc = routes_row[...], routes_col[...]
     onehot = hit(iota((NZ * NX, n_tok), 0), rr)
     ahead = jnp.where(iota((n_tok, n_tok), 0) < iota((n_tok, n_tok), 1), 1.0, 0.0).astype(BF)
     pos_r = jnp.sum(dot(onehot, ahead) * onehot.astype(F32), axis=0, keepdims=True).astype(jnp.int32)
@@ -109,27 +131,24 @@
 
     def tail_code(route, pos, i):
         high = jnp.where(pos >= 3, 1, 0)
-        return jnp.where(pos - 3 * high == i, route * MSG + 12 + high, -9)
+        return jnp.where(pos - 3 * high == i, route * MSG + CAP + high, -9)
 
     rows = NZ * NX * MSG
     q_id = iota((rows, n_tok), 0)
-    main_x = hit(q_id, rr * MSG + pos_r)
-    main_s = hit(q_id, rr * MSG + pos_r + CAP)
-
-    def columns(k, size):
-        part = slice(k, k + size)
+    main = hit(q_id, rr * MSG + pos_r)
+
+    def columns(i):
+        part = slice(i * third, (i + 1) * third)
         return tok[:, part], (gates[...] * cot[:, part].astype(F32)).astype(BF)
 
-    tail_x, tail_s = columns(3 * third, third)
+    tails = columns(3)
     for i in range(3):
-        code = tail_code(rr, pos_r, i)
-        choose = jnp.concatenate([main_x, main_s, hit(q_id, code), hit(q_id, code + 2)], axis=1)
-        part_x, part_s = columns(i * third, third)
-        data = jnp.concatenate([part_x, part_s, tail_x, tail_s], axis=0)
-        msend[:, :, i * third : (i + 1) * third] = (
-            dot(choose, data).astype(BF).reshape(NZ * NX, MSG, third)
-        )
-    mrecv[e] = msend[e]
+        choose = jnp.concatenate([main, hit(q_id, tail_code(rr, pos_r, i))], axis=1)
+        for out, now, tail in zip((send_x, send_s), columns(i), tails):
+            data = dot(choose, jnp.concatenate([now, tail], axis=0))
+            out[:, :, i * third : (i + 1) * third] = data.astype(BF).reshape(NZ * NX, MSG, third)
+    recv_x[e] = send_x[e]
+    recv_s[e] = send_s[e]
 
     pl.semaphore_wait(barrier, NZ * NX + 2)
 
@@ -175,14 +194,17 @@
             arrived((name, "down", 2), high)
             send((name, "mate", 2, 1), high, high, mate)
 
-    def ring_end(names):
+    def ring_end(names, near=True, far=True):
         d = 1 - c
         for name in names:
-            arrived((name, "mate"), halves[name][1].at[2 * y + d])
+            if near:
+                arrived((name, "mate"), halves[name][1].at[2 * y + d])
             for k in (0, 1):
-                arrived((name, "mate", 0, k), half(name, 2 * ym + d, k))
-                arrived((name, "mate", 1, k), half(name, 2 * yp + d, 1 - k))
-                arrived((name, "mate", 2, k), half(name, 2 * y2 + d, k))
+                if near:
+                    arrived((name, "mate", 0, k), half(name, 2 * ym + d, k))
+                    arrived((name, "mate", 1, k), half(name, 2 * yp + d, 1 - k))
+                if far:
+                    arrived((name, "mate", 2, k), half(name, 2 * y2 + d, k))
 
     ring_start(["h"])
     for j in range(1, NZ):
@@ -199,11 +221,24 @@
             device_id_type=MESH,
         )
 
-    ring_start(["g", "d"])
-
-    @pl.loop(1, NZ * NX)
-    def _(j):
-        token_copy(j, True, msend, mrecv, a_s, a_r).start()
+    def tokens_start(*copy):
+        @pl.loop(1, NZ * NX)
+        def _(j):
+            token_copy(j, True, *copy).start()
+
+    def tokens_wait(*copy):
+        @pl.loop(1, NZ * NX)
+        def _(j):
+            token_copy(j, False, *copy).wait_recv()
+
+    def tokens_sent(*copy):
+        @pl.loop(1, NZ * NX)
+        def _(j):
+            token_copy(j, True, *copy).wait_send()
+
+    ring_start(["d", "g"])
+    tokens_start(send_x, recv_x, x_s, x_r)
+    tokens_start(send_s, recv_s, s_s, s_r)
 
     ring_near(["h"], 0)
     ring_near(["h"], 1)
@@ -217,8 +252,9 @@
     for k in (0, 1):
         send(("x", "right", k), hw_half(x, k), hw_half(x, k), right)
         send(("x", "left", 1 - k), hw_half(x, 1 - k), hw_half(x, 1 - k), left)
+
     ring_far(["h"])
-    ring_near(["g", "d"], 0)
+    ring_near(["d", "g"], 0)
     arrived(("x", "right", 0), hw_half(xm, 0))
     send(("x", "right", 2), hw_half(xm, 0), hw_half(xm, 0), right)
     arrived(("x", "left", 1), hw_half(xp, 1))
@@ -228,8 +264,8 @@
     arrived(("x", "right", 2), hw_half(x2, 0))
     arrived(("x", "left", 2), hw_half(x2, 1))
     ring_end(["h"])
-    own_gu.wait()
-    own_dn.wait()
+    for copy in later_in:
+        copy.wait()
 
     n_dp = hxs.shape[0]
     n_all = n_dp * n_hot
@@ -337,29 +373,113 @@
     send(("gx", "sum", 0), hg_half(xp, 1), hgr_half(1, 1), right)
     send(("gx", "sum", 1), hg_half(xm, 0), hgr_half(2, 0), left)
 
-    ring_near(["g", "d"], 1)
+    ring_near(["d", "g"], 1)
     for yy in "2pmy":
         chip_add("h", yy)
     far_send("h")
     near_send("h", True)
 
-    @pl.loop(1, NZ * NX)
-    def _(j):
-        token_copy(j, False, msend, mrecv, a_s, a_r).wait_recv()
-
-    n_row = rxs.shape[0] // 2
-    col_id = iota((2 * n_row, rows), 1)
-    straight = hit(col_id, perm_col[:, 0:1])
-    tail = None
-    for i in range(3):
-        part = mrecv[:, :, i * third : (i + 1) * third].reshape(rows, third)
-        rxs[:, i * third : (i + 1) * third] = dot(straight, part).astype(BF)
-        piece = dot(hit(col_id, perm_col[:, i + 1 : i + 2]), part)
-        tail = piece if tail is None else tail + piece
-    rxs[:, 3 * third :] = tail.astype(BF)
+    n_row = rows
+    hidden = wdn.shape[0] * wdn.shape[1]
+    w_dn2 = wdn.reshape(hidden, width)
+    chip_rows = 2 * wgu.shape[1]
+    row_id, col_id = iota((rows, rows), 0), iota((rows, rows), 1)
+    kept = (iota((rows, 1), 0) & (MSG - 1)) < CAP
+
+    def spread_tail(a, b, i):
+        place = a & (MSG - 1)
+        return hit(b, jnp.where(place < CAP, tail_code(a >> 3, place, i), -9))
+
+    def rows_of(message, out):
+        tail = None
+        for i in range(3):
+            part = slice(i * third, (i + 1) * third)
+            data = message[:, :, part].reshape(rows, third)
+            out[:, part] = jnp.where(kept, data, jnp.zeros_like(data))
+            piece = dot(spread_tail(row_id, col_id, i), data)
+            tail = piece if tail is None else tail + piece
+        out[:, 3 * third :] = tail.astype(BF)
+
+    def message_of(data, out):
+        for i in range(3):
+            part = slice(i * third, (i + 1) * third)
+            moved = dot(spread_tail(col_id, row_id, i), data[:, 3 * third :])
+            out[:, :, part] = (
+                jnp.where(kept, data[:, part].astype(F32), moved).astype(BF).reshape(NZ * NX, MSG, third)
+            )
+
+    def act_block(yy, part):
+        ks = pl.ds(pl.multiple_of(CHIP[yy] * chip_rows, 128), chip_rows)
+        w = wgu[pl.ds(2 * CHIP[yy], 2), :, part].reshape(chip_rows, 256)
+        return dot(rx[:, ks], w)
+
+    tokens_wait(send_x, recv_x, x_s, x_r)
+    rows_of(recv_x, rx)
     for k in range(4):
         part = slice(k * third, (k + 1) * third)
-        xt[part] = rxs[0:n_row, part].T
+        xt[part] = rx[:, part].T
+    ring_end(["d", "g"], far=False)
+
+    @pl.loop(0, 2 * hidden // 256)
+    def _(n):
+        part = pl.ds(pl.multiple_of(n * 256, 256), 256)
+        acc[:, part] = act_block("y", part) + act_block("m", part) + act_block("p", part)
+
+    ring_far(["d"])
+    tokens_wait(send_s, recv_s, s_s, s_r)
+    rows_of(recv_s, rs)
+    ring_far(["g"])
+    ring_end(["d"], near=False)
+
+    @pl.loop(0, hidden // 256)
+    def _(n):
+        part = pl.ds(pl.multiple_of(n * 256, 256), 256)
+        dh_acc[:, part] = dot_nt(rs[...], w_dn2[part])
+
+    ring_end(["g"], near=False)
+
+    @pl.loop(0, hidden // 256)
+    def _(n):
+        first = pl.ds(pl.multiple_of(n * 256, 256), 256)
+        second = pl.ds(pl.multiple_of(hidden + n * 256, 256), 256)
+        g = acc[:, first] + act_block("2", first)
+        u = acc[:, second] + act_block("2", second)
+        dh = dh_acc[:, first]
+        s = 1.0 / (1.0 + jnp.exp(-g))
+        h = (g * s * u).astype(BF)
+        hid[:, first] = h
+        ht[first] = h.T
+        dact[:, first] = (dh * u * s * (1.0 + g * (1.0 - s))).astype(BF)
+        dact[:, second] = (dh * g * s).astype(BF)
+
+    half_rows = wgu.shape[1]
+
+    def grad_gu(yy):
+        lhs = xt[pl.ds(pl.multiple_of(CHIP[yy] * 2 * half_rows, 16), 2 * half_rows)]
+
+        @pl.loop(0, 2 * hidden // 256)
+        def _(n):
+            part = pl.ds(pl.multiple_of(n * 256, 256), 256)
+            both = dot(lhs, dact[:, part]).astype(BF)
+            pgu[pl.ds(2 * CHIP[yy], 2), :, part] = both.reshape(2, half_rows, 256)
+
+        chip_send("g", yy)
+
+    grad_gu("2")
+
+    @pl.loop(0, width // 256)
+    def _(n):
+        part = pl.ds(pl.multiple_of(n * 256, 256), 256)
+        pdn[:, :, part] = dot(ht[...], rs[:, part]).astype(BF).reshape(*pdn.shape[0:2], 256)
+
+    for yy in "2pmy":
+        chip_send("d", yy)
+    for name in "gd":
+        chip_add(name, "2")
+        far_send(name)
+
+    near_add("h")
+    near_send("h", False)
 
     arrived(("gx", "far", 0), hgr_half(0, 0))
     arrived(("gx", "far", 1), hgr_half(0, 1))
@@ -370,7 +490,33 @@
     send(("gx", "sum", 2), hg_half(xp, 0), hgr_half(1, 0), right)
     send(("gx", "sum", 3), hg_half(xm, 1), hgr_half(2, 1), left)
 
-    ring_far(["g", "d"])
+
+    @pl.loop(0, width // 256)
+    def _(n):
+        part = pl.ds(pl.multiple_of(n * 256, 256), 256)
+        rx[:, part] = dot(hid[...], w_dn2[:, part]).astype(BF)
+
+    tokens_sent(send_x, recv_x, x_s, x_r)
+    message_of(rx, send_x)
+    back_o[e] = send_x[e]
+    tokens_start(send_x, back_o, o_s, o_r)
+    grad_gu("p")
+    grad_gu("m")
+    for k in range(wgu.shape[0] // 2):
+        w = wgu[2 * k : 2 * k + 2].reshape(chip_rows, 2 * hidden)
+        rs[:, k * chip_rows : (k + 1) * chip_rows] = dot_nt(dact[...], w).astype(BF)
+    tokens_sent(send_s, recv_s, s_s, s_r)
+    message_of(rs, send_s)
+    back_g[e] = send_s[e]
+    tokens_start(send_s, back_g, g_s, g_r)
+    for yy in "pm":
+        for name in "gd":
+            chip_add(name, yy)
+    for name in "gd":
+        near_send(name, True)
+    for name in "gd":
+        near_add(name)
+        near_send(name, False)
     arrived(("gx", "sum", 0), hgr_half(1, 1))
     arrived(("gx", "sum", 1), hgr_half(2, 0))
     arrived(("gx", "sum", 2), hgr_half(1, 0))
@@ -383,136 +529,60 @@
     for j in range(1, NZ):
         there = (z + j) % NZ
         send(("gz", j), hg.at[there, x], hgz.at[z], (me, NX * there + x))
-    near_add("h")
-    near_send("h", False)
-    ring_end(["g", "d"])
-
-    hidden = wdn.shape[0] * wdn.shape[1]
-    model = wgu.shape[0] * wgu.shape[1]
-    w_dn2 = wdn.reshape(hidden, width)
-
-    @pl.loop(0, hidden // 256)
-    def _(n):
-        first = pl.ds(pl.multiple_of(n * 256, 256), 256)
-        second = pl.ds(pl.multiple_of(hidden + n * 256, 256), 256)
-        g = dot(rxs[0:n_row], wgu[:, :, first].reshape(model, 256))
-        u = dot(rxs[0:n_row], wgu[:, :, second].reshape(model, 256))
-        dh = dot_nt(rxs[n_row:], w_dn2[first])
-        s = 1.0 / (1.0 + jnp.exp(-g))
-        h = (g * s * u).astype(BF)
-        hid[:, first] = h
-        ht[first] = h.T
-        dact[:, first] = (dh * u * s * (1.0 + g * (1.0 - s))).astype(BF)
-        dact[:, second] = (dh * g * s).astype(BF)
-
-    half_rows = wgu.shape[1]
-
-    def grad_gu(yy):
-        lhs = xt[pl.ds(pl.multiple_of(CHIP[yy] * 2 * half_rows, 16), 2 * half_rows)]
-
-        @pl.loop(0, 2 * hidden // 256)
-        def _(n):
-            part = pl.ds(pl.multiple_of(n * 256, 256), 256)
-            both = dot(lhs, dact[:, part]).astype(BF)
-            pgu[pl.ds(2 * CHIP[yy], 2), :, part] = both.reshape(2, half_rows, 256)
-
-        chip_send("g", yy)
-
-    grad_gu("2")
-
-    @pl.loop(0, width // 256)
-    def _(n):
-        part = pl.ds(pl.multiple_of(n * 256, 256), 256)
-        pdn[:, :, part] = dot(ht[...], rxs[n_row:, part]).astype(BF).reshape(*pdn.shape[0:2], 256)
-
-    for yy in "2pmy":
-        chip_send("d", yy)
-    for name in "gd":
-        chip_add(name, "2")
-        far_send(name)
-
-    @pl.loop(0, width // 256)
-    def _(n):
-        part = pl.ds(pl.multiple_of(n * 256, 256), 256)
-        rxs[0:n_row, part] = dot(hid[...], w_dn2[:, part]).astype(BF)
-
-    for k in range(wgu.shape[0] // 2):
-        w = wgu[2 * k : 2 * k + 2].reshape(2 * half_rows, 2 * hidden)
-        rxs[n_row:, k * 2 * half_rows : (k + 1) * 2 * half_rows] = dot_nt(dact[...], w).astype(BF)
-
-    @pl.loop(1, NZ * NX)
-    def _(j):
-        token_copy(j, True, msend, mrecv, a_s, a_r).wait_send()
-
-    row_id = iota((rows, 2 * n_row), 0)
-    straight = hit(row_id, perm_row[0:1])
-    for i in range(3):
-        part = slice(i * third, (i + 1) * third)
-        mixed = dot(straight, rxs[:, part]) + dot(
-            hit(row_id, perm_row[i + 1 : i + 2]), rxs[:, 3 * third :]
-        )
-        msend[:, :, part] = mixed.astype(BF).reshape(NZ * NX, MSG, third)
-    mback[e] = msend[e]
-
-    @pl.loop(1, NZ * NX)
-    def _(j):
-        token_copy(j, True, msend, mback, b_s, b_r).start()
-
-    grad_gu("p")
-    grad_gu("m")
-    for yy in "pm":
-        for name in "gd":
-            chip_add(name, yy)
-    for name in "gd":
-        near_send(name, True)
     grad_gu("y")
     for name in "gd":
-        near_add(name)
-        near_send(name, False)
-    for name in "gd":
         chip_add(name, "y")
 
+    leaving = []
+    sum_wait("h")
+    hot_sum = qhb[y].astype(F32) + rhb[1].astype(F32) + rhb[2].astype(F32)
+    back = jnp.concatenate([hgate[...] * hot_sum[0:n_hot], hot_sum[n_hot:]], axis=1)
+    upper = back.astype(BF)
+    lower = (back - upper.astype(F32)).astype(BF)
+    spread = hit(iota((n_tok, n_hot), 0), hidx_row[...])
+
+    lane_id = iota((n_tok, rows), 1)
+    straight = hit(lane_id, rc * MSG + pos_c)
+    bent = [hit(lane_id, tail_code(rc, pos_c, i)) for i in range(3)]
+
+    def results(back_ref, hot_first, out):
+        tail = None
+        for i in range(4):
+            part = slice(i * third, (i + 1) * third)
+            if i < 3:
+                data = back_ref[:, :, part].reshape(rows, third)
+                got = dot(straight, data)
+                piece = dot(bent[i], data)
+                tail = piece if tail is None else tail + piece
+            else:
+                got = tail
+            lanes = slice(hot_first + i * third, hot_first + (i + 1) * third)
+            hot_part = dot(spread, upper[:, lanes]) + dot(spread, lower[:, lanes])
+            if hot_first == 0:
+                got = gates[...] * got
+            out[:, part] = (got + hot_part).astype(BF)
+
+    tokens_wait(send_x, back_o, o_s, o_r)
+    results(back_o, 0, lo_buf)
+    leaving.append(fetch(6, lo_buf, lo_out))
+    tokens_wait(send_s, back_g, g_s, g_r)
+    results(back_g, width, ig_buf)
+    leaving.append(fetch(7, ig_buf, ig_out))
+    scale = 1.0 / 32.0
     total = hgz[z].astype(F32)
     for j in range(1, NZ):
         there = (z + NZ - j) % NZ
         arrived(("gz", j), hgz.at[there])
         total = total + hgz[there].astype(F32)
-    scale = 1.0 / 32.0
-    ghw_out[...] = (total * scale).astype(BF)
-
-    sum_wait("h")
-    hot_sum = qhb[y].astype(F32) + rhb[1].astype(F32) + rhb[2].astype(F32)
-    back = jnp.concatenate([hgate[...] * hot_sum[0:n_hot], hot_sum[n_hot:]], axis=1)
-    upper = back.astype(BF)
-    back = jnp.concatenate([upper, (back - upper.astype(F32)).astype(BF)], axis=0)
-    spread = hit(iota((n_tok, 2 * n_hot), 0), hidx_row[...])
-
-    @pl.loop(1, NZ * NX)
-    def _(j):
-        token_copy(j, False, msend, mback, b_s, b_r).wait_recv()
-
-    lane_id = iota((n_tok, rows), 1)
-    code = rc * MSG + pos_c
-    straight = jnp.concatenate([hit(lane_id, code), hit(lane_id, code + CAP)], axis=0)
-    tail = None
-    for i in range(4):
-        part = slice(i * third, (i + 1) * third)
-        if i < 3:
-            data = mback[:, :, part].reshape(rows, third)
-            got = dot(straight, data)
-            code = tail_code(rc, pos_c, i)
-            piece = dot(
-                jnp.concatenate([hit(lane_id, code), hit(lane_id, code + 2)], axis=0), data
-            )
-            tail = piece if tail is None else tail + piece
-        else:
-            got = tail
-        hot_part = dot(spread, back[:, part])
-        hot_grad = dot(spread, back[:, width + i * third : width + (i + 1) * third])
-        lo_out[:, part] = (gates[...] * got[0:n_tok] + hot_part).astype(BF)
-        ig_out[:, part] = (got[n_tok:] + hot_grad).astype(BF)
-
-    for name, out in (("g", ggu_out), ("d", gdn_out)):
+    total = (total * scale).astype(BF)
+    ghg_buf[0] = total[:, 0:units]
+    ghg_buf[1] = total[:, 128 : 128 + units]
+    ghg_buf[2] = total[:, 256 : 256 + units]
+    leaving.append(fetch(8, ghg_buf.at[0:2], ghg_out))
+    leaving.append(fetch(9, ghg_buf.at[2], ghd_out))
+
+
+    for n, (name, out) in enumerate((("g", ggu_out), ("d", gdn_out))):
         _, q, r, size, step = sums[name]
         sum_wait(name)
 
@@ -520,26 +590,47 @@
         def _(i):
             part = pl.ds(pl.multiple_of(i * step, step), step)
             value = q[y, part].astype(F32) + r[1, part].astype(F32) + r[2, part].astype(F32)
-            out[0, part] = (value * scale).astype(BF)
+            q[y, part] = (value * scale).astype(BF)
+
+        leaving.append(fetch(n, q.at[y], out.at[0]))
 
     for copy in started:
         copy.wait_send()
-
-    @pl.loop(1, NZ * NX)
-    def _(j):
-        token_copy(j, True, msend, mback, b_s, b_r).wait_send()
-
-
-def row_tables(n_expert, n_row):
-    table = np.full((4, 2 * n_row), -1, np.int32)
-    for k in range(2):
-        for p in range(n_expert):
-            for r in range(CAP):
-                n = k * n_row + p * CAP + r
-                table[0, n] = p * MSG + k * CAP + r
-                place = k * CAP + r
-                table[1 + place % 3, n] = p * MSG + 12 + place // 3
-    return table
+    for copy in leaving:
+        copy.wait()
+
+    tokens_sent(send_x, back_o, o_s, o_r)
+    tokens_sent(send_s, back_g, g_s, g_r)
+
+
+def hand_over(*refs):
+    count = (len(refs) - 2) // 3
+    ins, outs, bufs = refs[:count], refs[count : 2 * count], refs[2 * count : 3 * count]
+    in_sem, out_sem = refs[3 * count :]
+    moves = []
+    for src, dst, buf in zip(ins, outs, bufs):
+        n = src.shape[-2] // 2
+        for k in range(2):
+            cut = (slice(None),) * (len(src.shape) - 2) + (slice(k * n, (k + 1) * n),)
+            if n % 16:
+                if k:
+                    continue
+                cut = ()
+            i = len(moves)
+            part = [r.at[cut] if cut else r for r in (src, buf, dst)]
+            moves.append(
+                (
+                    pltpu.make_async_copy(part[0], part[1], in_sem.at[i]),
+                    pltpu.make_async_copy(part[1], part[2], out_sem.at[i]),
+                )
+            )
+    for get, _ in moves:
+        get.start()
+    for get, put in moves:
+        get.wait()
+        put.start()
+    for _, put in moves:
+        put.wait()
 
 
 def local(
@@ -551,30 +642,34 @@
     rows_gu, double = w_gate_up.shape[1:]
     rows_dn = w_down.shape[1]
     units, features = w_hot_dn.shape
-    n_row = 256
-    table = row_tables(n_e, n_row)
-    perm_row = jnp.asarray(np.concatenate([table, np.full_like(table, -1)], axis=0))
-    perm_col = jnp.asarray(np.pad(table.T, ((0, 0), (0, 124)), constant_values=-1))
-    hot_w = jnp.concatenate([w_hot_gu, w_hot_dn[None]], axis=0)
-    hot_w = jnp.pad(hot_w, ((0, 0), (0, 128 - units), (0, 0))).transpose(2, 0, 1)
-    hot_w = hot_w.reshape(features, 384)
+    n_row = n_e * MSG
     vmem = pl.BlockSpec(memory_space=pltpu.VMEM)
     any_space = pl.BlockSpec(memory_space=pl.ANY)
     msg = (n_e, MSG, 3 * width // 4)
     hot2 = 2 * n_hot
     dma = pltpu.SemaphoreType.DMA
+    results = (
+        jax.ShapeDtypeStruct((n_tok, width), BF),
+        jax.ShapeDtypeStruct((n_tok, width), BF),
+        jax.ShapeDtypeStruct(w_gate_up.shape, BF),
+        jax.ShapeDtypeStruct(w_down.shape, BF),
+        jax.ShapeDtypeStruct((2, features, units), BF),
+        jax.ShapeDtypeStruct((features, units), BF),
+    )
     outs = pl.pallas_call(
         kernel,
-        out_shape=(
-            jax.ShapeDtypeStruct((n_tok, width), BF),
-            jax.ShapeDtypeStruct((n_tok, width), BF),
-            jax.ShapeDtypeStruct(w_gate_up.shape, BF),
-            jax.ShapeDtypeStruct(w_down.shape, BF),
-            jax.ShapeDtypeStruct(hot_w.shape, BF),
-        ),
-        in_specs=[vmem] * 10 + [any_space] * 2 + [vmem],
-        out_specs=(vmem,) * 5,
+        out_shape=results,
+        in_specs=[any_space] * 4 + [vmem] * 6,
+        out_specs=(any_space,) * 6,
         scratch_shapes=[
+            pltpu.VMEM((n_tok, width), BF),
+            pltpu.VMEM((n_tok, width), BF),
+            pltpu.VMEM((features, 384), BF),
+            pltpu.VMEM((n_tok, width), BF),
+            pltpu.VMEM((n_tok, width), BF),
+            pltpu.VMEM((3, features, units), BF),
+            pltpu.VMEM((n_tok, 1), F32),
+            pltpu.VMEM((n_hot, 1), F32),
             pltpu.VMEM((n_dp, rows_gu, double), BF),
             pltpu.VMEM((n_dp, rows_dn, width), BF),
             pltpu.VMEM((n_dp, hot2, width), BF),
@@ -582,11 +677,17 @@
             pltpu.VMEM(msg, BF),
             pltpu.VMEM(msg, BF),
             pltpu.VMEM(msg, BF),
-            pltpu.VMEM((2 * n_row, width), BF),
+            pltpu.VMEM(msg, BF),
+            pltpu.VMEM(msg, BF),
+            pltpu.VMEM(msg, BF),
+            pltpu.VMEM((n_row, width), BF),
+            pltpu.VMEM((n_row, width), BF),
             pltpu.VMEM((width, n_row), BF),
             pltpu.VMEM((double // 2, n_row), BF),
             pltpu.VMEM((n_row, double // 2), BF),
             pltpu.VMEM((n_row, double), BF),
+            pltpu.VMEM((n_row, double), F32),
+            pltpu.VMEM((n_row, double // 2), F32),
             pltpu.VMEM((n_dp, rows_gu, double), BF),
             pltpu.VMEM((n_dp, rows_dn, width), BF),
             pltpu.VMEM((n_dp, hot2, width), BF),
@@ -606,20 +707,32 @@
             dma((n_e,)),
             dma((n_e,)),
             dma((n_e,)),
-            dma((2,)),
+            dma((n_e,)),
+            dma((n_e,)),
+            dma((n_e,)),
+            dma((n_e,)),
+            dma((10,)),
         ],
         compiler_params=pltpu.CompilerParams(
             collective_id=0, has_side_effects=True, vmem_limit_bytes=67043328
         ),
         name="expert_layer",
     )(
-        tokens, cotangent, routes.reshape(1, n_tok), routes, gates,
-        jnp.tile(hot_index, 2).reshape(1, hot2), hot_index.reshape(n_hot, 1),
-        hot_gate.reshape(n_hot, 1), perm_col, perm_row, w_gate_up, w_down, hot_w,
+        tokens, cotangent, w_gate_up, w_down,
+        routes.reshape(1, n_tok), gates.reshape(1, n_tok),
+        hot_index.reshape(1, n_hot), hot_gate.reshape(1, n_hot),
+        w_hot_gu.transpose(0, 2, 1), w_hot_dn.T,
     )
-    layer_out, input_grad, grad_gu, grad_dn, grad_hot = outs
-    grad_hot = grad_hot.reshape(features, 3, 128)[:, :, :units].transpose(1, 2, 0)
-    return layer_out, input_grad, grad_gu, grad_dn, grad_hot[0:2], grad_hot[2]
+    outs = pl.pallas_call(
+        hand_over,
+        out_shape=results,
+        in_specs=[any_space] * 6,
+        out_specs=(any_space,) * 6,
+        scratch_shapes=[pltpu.VMEM(r.shape, BF) for r in results] + [dma((12,)), dma((12,))],
+        name="hand_over",
+    )(*outs)
+    layer_out, input_grad, grad_gu, grad_dn, hot_gu, hot_dn = outs
+    return layer_out, input_grad, grad_gu, grad_dn, hot_gu.transpose(0, 2, 1), hot_dn.T
 
 
 def solution(mesh):

time: 172 us -> 150 us (0.87)
  local copies, waits for them, and re-layouts: 13.4 us -> 0 us
  Pallas kernels: 156 us -> 148 us
    unnamed x22 -> x0, local copies, waits for them, and re-layouts: 8.33 us -> none
    pallas_call x1 -> x2, Pallas kernels: 156 us -> 148 us  [the longest x1 146 us: local(): pl.pallas_call(kernel, out_shape=results, in_specs=[any_space] * 4 + [vme...]
    reshape x3 -> x0, local copies, waits for them, and re-layouts: 3.51 us -> none  [the longest x1 1.33 us: local(): hot_gate.reshape(n_hot, 1)]
where the time goes in v2:
time: 150 us; the launch traced here: 149 us
  Pallas kernels  148 us (99%)
    pallas_call x1, Pallas kernels, local(): pl.pallas_call(kernel, out_shape=results, in_specs=[any_space] * 4 + [vme...  146 us

profile of v2, /device:TPU:7, one launch (start us, length us, event | category | flops | bytes accessed | tf_op | source)
XLA Modules:
  0.0 149.0 jit_solution(8598890860796267007)
XLA Ops:
  0.6 145.6 %expert_layer.1 = (bf16[128,2560]{1,0:T(8,128)(2,1)}, bf16[128,2560]{1,0:T(8,128)(2,1)}, bf16[1,320,1536]{2,1,0:T(8,128)(2,1)}, bf16[1,96,2560]{2,1,0:T(8,128)(2...) custom-call(bf16[128,2560]{1,0:T(8,128)(2,1)} %tok_in.1, bf16[128,2560]{1,0:T(8,128)(2,1)} %cot_in.1, ...), custom_call_target="tpu_custom_call" | custom-call | tf_op jit(solution)/shard_map/expert_layer/pallas_call | solution.py:659
  146.3 2.7 %hand_over.1 = (bf16[128,2560]{1,0:T(8,128)(2,1)}, bf16[128,2560]{1,0:T(8,128)(2,1)}, bf16[1,320,1536]{2,1,0:T(8,128)(2,1)}, bf16[1,96,2560]{2,1,0:T(8,128)(2,1)...) custom-call(bf16[128,2560]{1,0:T(8,128)(2,1)} %get-tuple-element.18.refs_0_, ...), custom_call_target="tpu_custom_call" | custom-call | tf_op jit(solution)/shard_map/hand_over/pallas_call | solution.py:726

commit v3 on v2

--- a/solution.py
+++ b/solution.py
@@ -238,7 +238,6 @@
 
     ring_start(["d", "g"])
     tokens_start(send_x, recv_x, x_s, x_r)
-    tokens_start(send_s, recv_s, s_s, s_r)
 
     ring_near(["h"], 0)
     ring_near(["h"], 1)
@@ -252,7 +251,7 @@
     for k in (0, 1):
         send(("x", "right", k), hw_half(x, k), hw_half(x, k), right)
         send(("x", "left", 1 - k), hw_half(x, 1 - k), hw_half(x, 1 - k), left)
-
+    tokens_start(send_s, recv_s, s_s, s_r)
     ring_far(["h"])
     ring_near(["d", "g"], 0)
     arrived(("x", "right", 0), hw_half(xm, 0))
@@ -425,6 +424,15 @@
         part = pl.ds(pl.multiple_of(n * 256, 256), 256)
         acc[:, part] = act_block("y", part) + act_block("m", part) + act_block("p", part)
 
+    arrived(("gx", "far", 0), hgr_half(0, 0))
+    arrived(("gx", "far", 1), hgr_half(0, 1))
+    for k, col in ((0, xp), (1, xm)):
+        for i in range(NZ // 2):
+            n = k * (NZ // 2) + i
+            hg[n, col] = (hg[n, col].astype(F32) + hgr[0, n].astype(F32)).astype(BF)
+    send(("gx", "sum", 2), hg_half(xp, 0), hgr_half(1, 0), right)
+    send(("gx", "sum", 3), hg_half(xm, 1), hgr_half(2, 1), left)
+
     ring_far(["d"])
     tokens_wait(send_s, recv_s, s_s, s_r)
     rows_of(recv_s, rs)
@@ -436,6 +444,8 @@
         part = pl.ds(pl.multiple_of(n * 256, 256), 256)
         dh_acc[:, part] = dot_nt(rs[...], w_dn2[part])
 
+    near_add("h")
+    near_send("h", False)
     ring_end(["g"], near=False)
 
     @pl.loop(0, hidden // 256)
@@ -466,6 +476,31 @@
         chip_send("g", yy)
 
     grad_gu("2")
+    arrived(("gx", "sum", 0), hgr_half(1, 1))
+    arrived(("gx", "sum", 1), hgr_half(2, 0))
+    arrived(("gx", "sum", 2), hgr_half(1, 0))
+    arrived(("gx", "sum", 3), hgr_half(2, 1))
+    for n in range(NZ):
+        hg[n, x] = (
+            hg[n, x].astype(F32) + hgr[1, n].astype(F32) + hgr[2, n].astype(F32)
+        ).astype(BF)
+    hgz[z] = hg[z, x]
+    for j in range(1, NZ):
+        there = (z + j) % NZ
+        send(("gz", j), hg.at[there, x], hgz.at[z], (me, NX * there + x))
+
+    @pl.loop(0, width // 256)
+    def _(n):
+        part = pl.ds(pl.multiple_of(n * 256, 256), 256)
+        rx[:, part] = dot(hid[...], w_dn2[:, part]).astype(BF)
+
+    chip_add("g", "2")
+    far_send("g")
+
+    tokens_sent(send_x, recv_x, x_s, x_r)
+    message_of(rx, send_x)
+    back_o[e] = send_x[e]
+    tokens_start(send_x, back_o, o_s, o_r)
 
     @pl.loop(0, width // 256)
     def _(n):
@@ -474,33 +509,9 @@
 
     for yy in "2pmy":
         chip_send("d", yy)
-    for name in "gd":
-        chip_add(name, "2")
-        far_send(name)
-
-    near_add("h")
-    near_send("h", False)
-
-    arrived(("gx", "far", 0), hgr_half(0, 0))
-    arrived(("gx", "far", 1), hgr_half(0, 1))
-    for k, col in ((0, xp), (1, xm)):
-        for i in range(NZ // 2):
-            n = k * (NZ // 2) + i
-            hg[n, col] = (hg[n, col].astype(F32) + hgr[0, n].astype(F32)).astype(BF)
-    send(("gx", "sum", 2), hg_half(xp, 0), hgr_half(1, 0), right)
-    send(("gx", "sum", 3), hg_half(xm, 1), hgr_half(2, 1), left)
-
-
-    @pl.loop(0, width // 256)
-    def _(n):
-        part = pl.ds(pl.multiple_of(n * 256, 256), 256)
-        rx[:, part] = dot(hid[...], w_dn2[:, part]).astype(BF)
-
-    tokens_sent(send_x, recv_x, x_s, x_r)
-    message_of(rx, send_x)
-    back_o[e] = send_x[e]
-    tokens_start(send_x, back_o, o_s, o_r)
     grad_gu("p")
+    chip_add("d", "2")
+    far_send("d")
     grad_gu("m")
     for k in range(wgu.shape[0] // 2):
         w = wgu[2 * k : 2 * k + 2].reshape(chip_rows, 2 * hidden)
@@ -517,18 +528,6 @@
     for name in "gd":
         near_add(name)
         near_send(name, False)
-    arrived(("gx", "sum", 0), hgr_half(1, 1))
-    arrived(("gx", "sum", 1), hgr_half(2, 0))
-    arrived(("gx", "sum", 2), hgr_half(1, 0))
-    arrived(("gx", "sum", 3), hgr_half(2, 1))
-    for n in range(NZ):
-        hg[n, x] = (
-            hg[n, x].astype(F32) + hgr[1, n].astype(F32) + hgr[2, n].astype(F32)
-        ).astype(BF)
-    hgz[z] = hg[z, x]
-    for j in range(1, NZ):
-        there = (z + j) % NZ
-        send(("gz", j), hg.at[there, x], hgz.at[z], (me, NX * there + x))
     grad_gu("y")
     for name in "gd":
         chip_add(name, "y")

time: 150 us -> 148 us (0.987)
  Pallas kernels: 148 us -> 146 us
    pallas_call x1, Pallas kernels: 146 us -> 143 us  [local(): pl.pallas_call(kernel, out_shape=results, in_specs=[any_space] * 4 + [vme...]
where the time goes in v3:
time: 148 us; the launch traced here: 146 us
  Pallas kernels  146 us (99%)
    pallas_call x1, Pallas kernels, local(): pl.pallas_call(kernel, out_shape=results, in_specs=[any_space] * 4 + [vme...  143 us

profile of v3, /device:TPU:7, one launch (start us, length us, event | category | flops | bytes accessed | tf_op | source)
XLA Modules:
  0.0 146.3 jit_solution(12590924280969088951)
XLA Ops:
  0.6 143.0 %expert_layer.1 = (bf16[128,2560]{1,0:T(8,128)(2,1)}, bf16[128,2560]{1,0:T(8,128)(2,1)}, bf16[1,320,1536]{2,1,0:T(8,128)(2,1)}, bf16[1,96,2560]{2,1,0:T(8,128)(2...) custom-call(bf16[128,2560]{1,0:T(8,128)(2,1)} %tok_in.1, bf16[128,2560]{1,0:T(8,128)(2,1)} %cot_in.1, ...), custom_call_target="tpu_custom_call" | custom-call | tf_op jit(solution)/shard_map/expert_layer/pallas_call | solution.py:658
  143.6 2.7 %hand_over.1 = (bf16[128,2560]{1,0:T(8,128)(2,1)}, bf16[128,2560]{1,0:T(8,128)(2,1)}, bf16[1,320,1536]{2,1,0:T(8,128)(2,1)}, bf16[1,96,2560]{2,1,0:T(8,128)(2,1)...) custom-call(bf16[128,2560]{1,0:T(8,128)(2,1)} %get-tuple-element.18.refs_0_, ...), custom_call_target="tpu_custom_call" | custom-call | tf_op jit(solution)/shard_map/hand_over/pallas_call | solution.py:725
